TPU v7x, 768 devices: a whole 4x8x12 slice. The times are simulated.
768 devices in a mesh: grp: 24 (over z, core), sub: 32 (over x, y).
Axes of the slice: x: 4, y: 8, z: 12, core: 2. Of those that a mesh axis runs over, the one named last changes fastest.
Arguments:
- residual4: float32 [128, 96, 128], P(None, 'grp', 'sub'), may hold values from -6 to 6
- spacing: float32 [128], replicated, may hold values from 0.5 to 2
Outputs:
- correction: float32 [128, 96, 128], P(None, 'grp', 'sub')
- coarse_solution: float32 [64, 48, 64], P(None, 'grp', 'sub')
All inputs are finite; a program needn't handle non-finite values.
Results may differ from a plain program's by a relative error of at most 0.00026.
Values sent between devices are 32-bit elements; how exact they have to be, the bound alone decides.
A program may use at most 64 MiB of HBM per device.

v0:
```python
import math

import jax
import jax.numpy as jnp
from jax import lax
from jax.sharding import PartitionSpec as P

SWEEPS = 2


highest = lax.Precision.HIGHEST
damping = 0.8


def padded(cells, sides, width):
    for axis, dim in sides:
        count = lax.axis_size(axis)
        head = lax.slice_in_dim(cells, 0, width, axis=dim)
        tail = lax.slice_in_dim(cells, cells.shape[dim] - width, cells.shape[dim], axis=dim)
        cells = jnp.concatenate(
            [
                lax.ppermute(tail, axis, [(i, (i + 1) % count) for i in range(count)]),
                cells,
                lax.ppermute(head, axis, [((i + 1) % count, i) for i in range(count)]),
            ],
            axis=dim,
        )
    return cells


def couplings(spacing):
    face_coef = 2.0 / (spacing[:-1] + spacing[1:])
    zero_end = jnp.zeros((1,), spacing.dtype)
    upper_face = jnp.concatenate([face_coef, zero_end])
    lower_face = jnp.concatenate([zero_end, face_coef])
    return (upper_face, lower_face)


def column(vector):
    return vector[:, None, None]


def apply_operator(grid_field, spacing, upper_face, lower_face):
    centre = grid_field[:, 1:-1, :]
    west_side = jnp.roll(centre, 1, 2)
    east_side = jnp.roll(centre, -1, 2)
    south_side = grid_field[:, :-2, :]
    north_side = grid_field[:, 2:, :]
    zero_layer = jnp.zeros_like(centre[:1])
    above_cell = jnp.concatenate([centre[1:], zero_layer], 0)
    below_cell = jnp.concatenate([zero_layer, centre[:-1]], 0)
    inplane = column(spacing) * (4.0 * centre - west_side - east_side - south_side - north_side)
    vertical = column(upper_face) * (centre - above_cell) + column(lower_face) * (
        centre - below_cell
    )
    return inplane + vertical


def tables(count, span, offset):
    wavenum = lax.broadcasted_iota(jnp.int32, (count, span), 0)
    position = lax.broadcasted_iota(jnp.int32, (count, span), 1) + offset
    phase_angle = 2.0 * math.pi / count * (wavenum * position % count).astype(jnp.float32)
    return (jnp.cos(phase_angle), jnp.sin(phase_angle))


def solve_columns(real_part, imag_part, spacing5, eigen_xy, anchor):
    upper5, lower5 = couplings(spacing5)
    levels_z = spacing5.shape[0]
    factor_prev = jnp.zeros_like(eigen_xy)
    value_re = jnp.zeros_like(real_part[0])
    value_im = jnp.zeros_like(imag_part[0])
    factor_list = []
    re_list = []
    im_list = []
    for level in range(levels_z):
        flag_k = 1.0 if level == 0 else 0.0
        coef_up = upper5[level]
        coef_low = lower5[level]
        pivot = (
            eigen_xy * spacing5[level]
            + coef_up
            + coef_low
            + flag_k * anchor
            + coef_low * factor_prev
        )
        factor_prev = -coef_up / pivot
        value_re = (real_part[level] + coef_low * value_re) / pivot
        value_im = (imag_part[level] + coef_low * value_im) / pivot
        factor_list.append(factor_prev)
        re_list.append(value_re)
        im_list.append(value_im)
    next_re = jnp.zeros_like(real_part[0])
    next_im = jnp.zeros_like(imag_part[0])
    solved_re = [None] * levels_z
    solved_im = [None] * levels_z
    for level in range(levels_z - 1, -1, -1):
        next_re = re_list[level] - factor_list[level] * next_re
        next_im = im_list[level] - factor_list[level] * next_im
        solved_re[level] = next_re
        solved_im[level] = next_im
    return (jnp.stack(solved_re, 0), jnp.stack(solved_im, 0))


def mode_solve(real_part, imag_part, spacing5, ny5, nx5):
    span_a = real_part.shape[2]
    wave_b = lax.broadcasted_iota(jnp.int32, (ny5, span_a), 0)
    wave_a = lax.broadcasted_iota(jnp.int32, (ny5, span_a), 1)
    anchor = ((wave_b == 0) & (wave_a == 0)).astype(jnp.float32)
    real_part = real_part - anchor[None] * jnp.mean(real_part[:, 0, 0])
    imag_part = imag_part - anchor[None] * jnp.mean(imag_part[:, 0, 0])
    eigen_xy = 0.25 * (
        2.0
        - 2.0 * jnp.cos(2.0 * math.pi * wave_a.astype(jnp.float32) / nx5)
        + (2.0 - 2.0 * jnp.cos(2.0 * math.pi * wave_b.astype(jnp.float32) / ny5))
    )
    return solve_columns(real_part, imag_part, spacing5, eigen_xy, anchor)


def on_device(residual4, spacing):
    sweeps = SWEEPS
    upper_face, lower_face = couplings(spacing)
    diagonal = column(4.0 * spacing + upper_face + lower_face)
    n_grp = lax.axis_size("grp")
    own_x = residual4.shape[2]
    source = lax.all_gather(residual4, "sub", axis=2, tiled=True)

    def extend(grid_field, margin):
        return padded(grid_field, (("grp", 1),), margin)

    def operate(grid_field):
        return apply_operator(grid_field, spacing, upper_face, lower_face)

    smooth = damping * source / diagonal
    smooth = smooth + damping * (source - operate(extend(smooth, 1))) / diagonal
    leftover = source - operate(extend(smooth, 1))
    levels_z, rows_y, cols_x = leftover.shape
    coarse = (
        leftover.reshape(levels_z // 2, 2, rows_y // 2, 2, cols_x // 2, 2).sum(axis=(1, 3, 5)) / 4.0
    )
    nz5, part_rows, nx5 = coarse.shape
    ny5 = part_rows * n_grp
    cos_x, sin_x = tables(nx5, nx5, 0)
    spacing5 = spacing.reshape(levels_z // 2, 2).sum(axis=1)
    cos_own, sin_own = tables(ny5, part_rows, lax.axis_index("grp") * part_rows)
    empty_sum = jnp.zeros((nz5, ny5, nx5), jnp.float32)
    portion = lax.all_gather(coarse, "grp", axis=1, tiled=True)
    imag_sum = empty_sum
    cos_y, sin_y = tables(ny5, portion.shape[1], jnp.int32(0))
    along_c = jnp.einsum("zyx,ax->zya", portion, cos_x, precision=highest)
    along_s = jnp.einsum("zyx,ax->zya", portion, sin_x, precision=highest)
    real_sum = jnp.einsum("zya,by->zba", along_c, cos_y, precision=highest) - jnp.einsum(
        "zya,by->zba", along_s, sin_y, precision=highest
    )
    imag_sum = (
        imag_sum
        - jnp.einsum("zya,by->zba", along_c, sin_y, precision=highest)
        - jnp.einsum("zya,by->zba", along_s, cos_y, precision=highest)
    )
    solved_re, solved_im = mode_solve(real_sum, imag_sum, spacing5, ny5, nx5)
    back_c = jnp.einsum("zba,by->zya", solved_re, cos_own, precision=highest) - jnp.einsum(
        "zba,by->zya", solved_im, sin_own, precision=highest
    )
    back_s = jnp.einsum("zba,by->zya", solved_re, sin_own, precision=highest) + jnp.einsum(
        "zba,by->zya", solved_im, cos_own, precision=highest
    )
    cos_use, sin_use = (cos_x, sin_x)
    coarse_part = (
        jnp.einsum("zya,ax->zyx", back_c, cos_use, precision=highest)
        - jnp.einsum("zya,ax->zyx", back_s, sin_use, precision=highest)
    ) / (nx5 * ny5)
    lifted = smooth + jnp.repeat(jnp.repeat(jnp.repeat(coarse_part, 2, 0), 2, 1), 2, 2)
    for sweep_no in range(sweeps):
        lifted = lifted + damping * (source - operate(extend(lifted, 1))) / diagonal
    sub_index = lax.axis_index("sub")
    correction = lax.dynamic_slice_in_dim(lifted, sub_index * own_x, own_x, 2)
    coarse_solution = lax.dynamic_slice_in_dim(coarse_part, sub_index * (own_x // 2), own_x // 2, 2)
    return (correction, coarse_solution)


def solution(mesh):
    placed = (P(None, "grp", "sub"), P())
    return jax.shard_map(
        on_device,
        mesh=mesh,
        in_specs=placed,
        out_specs=(P(None, "grp", "sub"), P(None, "grp", "sub")),
        check_vma=False,
    )
```

profile of v0, /device:TPU:1, one launch (start us, length us, event | category | flops | bytes accessed | tf_op | source)
XLA Modules:
  0.0 811.3 jit_solution(7934855802111142143)
XLA Ops:
  2.1 39.2 %all_gather.6 = f32[128,4,128]{0,1,2:T(4,128)S(1)} all-gather(f32[128,4,4]{0,1,2:T(4,128)S(1)} %copy.19), channel_id=1, replica_groups=mesh['grp'=24,'sub'=32] {'sub'}, dimensions={2}, use_global_device_ids=true | all-gather | bytes 270336 | tf_op jit(solution)/shard_map/all_gather | solution.py:125
  42.2 14.7 %collective-permute-start = (f32[128,1,128]{0,1,2:T(1,128)S(1)}, f32[128,1,128]{0,1,2:T(1,128)S(1)}, u32[]{:S(2)}, u32[]{:S(2)}) collective-permute-start(f32[128,1,128]{0,1,2:T(1,128)S(1)} %get-tuple-element.151), channel_id=1, source_target_pairs={{0,32},{32,64},{64,96},{96,128},{128,160},{160,192},{192,224},{224... | collective-permute-start | bytes 196616 | tf_op jit(solution)/shard_map/ppermute | solution.py:22
  56.9 2.7 collective-permute-start.1
  146.1 2.9 collective-permute-start.3
  150.6 18.1 %reshape.7090 = f32[64,2,2,2,64,2]{5,4,1,0,3,2:T(8,128)} reshape(f32[128,4,128]{2,0,1:T(8,128)S(1)} %copy.20) | data formatting | bytes 524288 | tf_op jit(solution)/shard_map/reshape | solution.py:138
  168.7 7.0 reduce_sum.36
  175.7 34.3 %all_gather.7 = f32[64,48,64]{2,0,1:T(8,128)S(1)} all-gather(f32[64,2,64]{2,0,1:T(8,128)S(1)} %broadcast_multiply_fusion), channel_id=1, replica_groups=mesh['grp'=24,'sub'=32] {'grp'}, dimensions={1}, use_global_device_ids=true | all-gather | bytes 819200 | tf_op jit(solution)/shard_map/all_gather | solution.py:146
  210.0 2.5 fusion.2
  212.5 2.5 fusion
  220.5 2.8 subtract_bitcast_fusion
  228.0 15.7 %add_divide_fusion.17 = (f32[1,48,64]{2,1,0:T(8,128)S(1)}, f32[1,48,64]{2,1,0:T(8,128)S(1)}, f32[1,48,64]{2,1,0:T(8,128)S(1)}, f32[1,48,64]{2,1,0:T(8,128)S(1)},...) fusion(f32[64,48,64]{2,1,0:T(8,128)S(1)} %get-tuple-element.296, ...), kind=kLoop, calls=%fused_computation.1079 | loop fusion | flops 657408 | bytes 418636 | tf_op jit(solution)/shard_map/div | solution.py:88
  243.7 15.5 %add_divide_fusion.56 = (f32[1,48,64]{2,1,0:T(8,128)S(1)}, f32[1,48,64]{2,1,0:T(8,128)S(1)}, f32[1,48,64]{2,1,0:T(8,128)S(1)}, f32[1,48,64]{2,1,0:T(8,128)S(1)},...) fusion(f32[64,48,64]{2,1,0:T(8,128)S(1)} %get-tuple-element.297, ...), kind=kLoop, calls=%fused_computation.1178 | loop fusion | flops 657408 | bytes 418636 | tf_op jit(solution)/shard_map/div | solution.py:87
  259.3 28.1 %fusion.384 = (f32[48,64]{1,0:T(8,128)S(1)}, f32[48,64]{1,0:T(8,128)S(1)}, f32[48,64]{1,0:T(8,128)S(1)}, f32[48,64]{1,0:T(8,128)S(1)}, f32[48,64]{1,0:T(8,128)S(...) fusion(f32[64,48,64]{2,1,0:T(8,128)S(1)} %get-tuple-element.296, ...), kind=kLoop, calls=%fused_computation.674 | loop fusion | flops 1210368 | bytes 652348 | tf_op jit(solution)/shard_map/div | solution.py:88
  287.4 28.1 %fusion.532 = (f32[48,64]{1,0:T(8,128)S(1)}, f32[48,64]{1,0:T(8,128)S(1)}, f32[48,64]{1,0:T(8,128)S(1)}, f32[48,64]{1,0:T(8,128)S(1)}, f32[48,64]{1,0:T(8,128)S(1)}, /*index=5*/f32[48,64]{1,0:T(8,128)S(1)}) fusion(f32[64,48,64]{2,1,0:T(8,128)S(1)} %get-tuple-element.297, f32[]{:T(128)} %bitcast.137, f32[]{:T(128)} %bitcast.136, f32[]{:T(128)} %bitcast.134, ...), kind=kLoop, calls=%fused_computation.933 | loop fusion | flops 1155072 | bytes 652324 | tf_op jit(solution)/shard_map/div | solution.py:87
  315.5 42.2 %constant_dynamic-update-slice_fusion.127 = (f32[64,48,64]{2,1,0:T(8,128)S(1)}, f32[48,64]{1,0:T(8,128)S(1)}, f32[48,64]{1,0:T(8,128)S(1)}, f32[48,64]{1,0:T(8,1...) fusion(pred[64]{0:T(512)(128)(4,1)S(1)} %iota_compare_fusion, ...), kind=kLoop, calls=%fused_computation.247 | loop fusion | flops 2055167 | bytes 1266972
  357.6 41.9 %constant_dynamic-update-slice_fusion.63 = (f32[64,48,64]{2,1,0:T(8,128)S(1)}, f32[48,64]{1,0:T(8,128)S(1)}, f32[48,64]{1,0:T(8,128)S(1)}, f32[48,64]{1,0:T(8,12...) fusion(pred[64]{0:T(512)(128)(4,1)S(1)} %iota_compare_fusion, ...), kind=kLoop, calls=%fused_computation.183 | loop fusion | flops 2042879 | bytes 1217804
  399.5 43.8 %constant_dynamic-update-slice_fusion.125 = (f32[64,48,64]{2,1,0:T(8,128)S(1)}, f32[1,48,64]{2,1,0:T(8,128)S(1)}, f32[1,48,64]{2,1,0:T(8,128)S(1)}, f32[1,48,64]...) fusion(f32[64,48,64]{2,1,0:T(8,128)S(1)} %constant_dynamic-upda, ...), kind=kLoop, calls=%fused_computation.245 | loop fusion | flops 2052096 | bytes 2397184
  443.3 42.0 %constant_dynamic-update-slice_fusion.61 = (f32[64,48,64]{2,1,0:T(8,128)S(1)}, f32[1,48,64]{2,1,0:T(8,128)S(1)}, f32[1,48,64]{2,1,0:T(8,128)S(1)}, f32[1,48,64]{...) fusion(f32[64,48,64]{2,1,0:T(8,128)S(1)} %constant_dynamic-upda, ...), kind=kLoop, calls=%fused_computation.181 | loop fusion | flops 1990656 | bytes 2395136
  485.4 2.6 constant_dynamic-update-slice_fusion.60
  488.0 4.0 constant_dynamic-update-slice_fusion.58
  492.0 5.2 constant_dynamic-update-slice_fusion.56
  497.3 6.5 constant_dynamic-update-slice_fusion.54
  503.8 7.8 constant_dynamic-update-slice_fusion.52
  511.6 9.1 %constant_dynamic-update-slice_fusion.50 = f32[64,48,64]{2,1,0:T(8,128)S(1)} fusion(f32[64,48,64]{2,1,0:T(8,128)S(1)} %constant_dynamic-update-slice_fusion.51, f32[1,48,64]{2,1,0:T(8,128)S(1)} %get-tuple-element.92, f32[1,48,64]{2,1,0:T(8,128)S(1)} %get-tuple-element.72, pred[64]{0:T(512)(128)(4,1)S(1)} %iota_compare_fusion, ...), kind=kLoop, calls=%fused_computation.170 | loop fusion | flops 267264 | bytes 75944
  520.8 10.3 %constant_dynamic-update-slice_fusion.48 = f32[64,48,64]{2,1,0:T(8,128)S(1)} fusion(f32[64,48,64]{2,1,0:T(8,128)S(1)} %constant_dynamic-update-slice_fusion.49, f32[1,48,64]{2,1,0:T(8,128)S(1)} %get-tuple-element.91, f32[1,48,64]{2,1,0:T(8,128)S(1)} %get-tuple-element.73, pred[64]{0:T(512)(128)(4,1)S(1)} %iota_compare_fusion, ...), kind=kLoop, calls=%fused_computation.168 | loop fusion | flops 304128 | bytes 75968
  531.1 11.7 %constant_dynamic-update-slice_fusion.46 = f32[64,48,64]{2,1,0:T(8,128)S(1)} fusion(f32[64,48,64]{2,1,0:T(8,128)S(1)} %constant_dynamic-update-slice_fusion.47, f32[1,48,64]{2,1,0:T(8,128)S(1)} %get-tuple-element.74, pred[64]{0:T(512)(128)(4,1)S(1)} %iota_compare_fusion, pred[48]{0:T(512)(128)(4,1)S(1)} %iota_compare_fusion.1, f32[]{:T(128)} %bitcast.7, ...), kind=kLoop, calls=%fused_computation.166 | loop fusion | flops 359424 | bytes 125144
  542.8 13.6 %constant_dynamic-update-slice_fusion.44 = f32[64,48,64]{2,1,0:T(8,128)S(1)} fusion(f32[64,48,64]{2,1,0:T(8,128)S(1)} %constant_dynamic-update-slice_fusion.45, f32[1,48,64]{2,1,0:T(8,128)S(1)} %get-tuple-element.90, pred[64]{0:T(512)(128)(4,1)S(1)} %iota_compare_fusion, pred[48]{0:T(512)(128)(4,1)S(1)} %iota_compare_fusion.1, f32[]{:T(128)} %bitcast.7, ...), kind=kLoop, calls=%fused_computation.164 | loop fusion | flops 411648 | bytes 100604
  556.4 13.6 %constant_dynamic-update-slice_fusion.43 = f32[64,48,64]{2,1,0:T(8,128)S(1)} fusion(f32[64,48,64]{2,1,0:T(8,128)S(1)} %constant_dynamic-update-slice_fusion.44, f32[1,48,64]{2,1,0:T(8,128)S(1)} %get-tuple-element.75, f32[]{:T(128)S(6)} %neg.209, pred[64]{0:T(512)(128)(4,1)S(1)} %iota_compare_fusion, pred[48]{0:T(512)(128)(4,1)S(1)} %iota_compare_fusion.1, ...), kind=kLoop, calls=%fused_computation.163 | loop fusion | flops 405504 | bytes 100604
  570.0 14.9 %constant_dynamic-update-slice_fusion.41 = f32[64,48,64]{2,1,0:T(8,128)S(1)} fusion(f32[64,48,64]{2,1,0:T(8,128)S(1)} %constant_dynamic-update-slice_fusion.42, f32[1,48,64]{2,1,0:T(8,128)S(1)} %get-tuple-element.76, f32[]{:T(128)S(6)} %neg.211, f32[]{:T(128)S(6)} %neg.210, f32[]{:T(128)} %bitcast.71, f32[]{:T(128)} %bitcast.74, f32[]{:T(128)} %bitcast.73, ...), kind=kLoop, calls=%fused_computation.161 | loop fusion | flops 442368 | bytes 100628
  584.9 2.6 constant_dynamic-update-slice_fusion.124
  587.6 4.0 constant_dynamic-update-slice_fusion.122
  591.6 5.2 constant_dynamic-update-slice_fusion.120
  596.8 6.5 constant_dynamic-update-slice_fusion.118
  603.3 7.8 constant_dynamic-update-slice_fusion.116
  611.1 9.1 %constant_dynamic-update-slice_fusion.114 = f32[64,48,64]{2,1,0:T(8,128)S(1)} fusion(f32[64,48,64]{2,1,0:T(8,128)S(1)} %constant_dynamic-update-slice_fusion.115, f32[1,48,64]{2,1,0:T(8,128)S(1)} %get-tuple-element.33, f32[1,48,64]{2,1,0:T(8,128)S(1)} %get-tuple-element.10, pred[64]{0:T(512)(128)(4,1)S(1)} %iota_compare_fusion, ...), kind=kLoop, calls=%fused_computation.234 | loop fusion | flops 267264 | bytes 75944
  620.3 10.3 %constant_dynamic-update-slice_fusion.112 = f32[64,48,64]{2,1,0:T(8,128)S(1)} fusion(f32[64,48,64]{2,1,0:T(8,128)S(1)} %constant_dynamic-update-slice_fusion.113, f32[1,48,64]{2,1,0:T(8,128)S(1)} %get-tuple-element.32, f32[1,48,64]{2,1,0:T(8,128)S(1)} %get-tuple-element.11, pred[64]{0:T(512)(128)(4,1)S(1)} %iota_compare_fusion, ...), kind=kLoop, calls=%fused_computation.232 | loop fusion | flops 304128 | bytes 75968
  630.6 11.7 %constant_dynamic-update-slice_fusion.110 = f32[64,48,64]{2,1,0:T(8,128)S(1)} fusion(f32[64,48,64]{2,1,0:T(8,128)S(1)} %constant_dynamic-update-slice_fusion.111, f32[1,48,64]{2,1,0:T(8,128)S(1)} %get-tuple-element.12, pred[64]{0:T(512)(128)(4,1)S(1)} %iota_compare_fusion, pred[48]{0:T(512)(128)(4,1)S(1)} %iota_compare_fusion.1, f32[]{:T(128)} %bitcast.7, ...), kind=kLoop, calls=%fused_computation.230 | loop fusion | flops 359424 | bytes 125144
  642.3 13.6 %constant_dynamic-update-slice_fusion.108 = f32[64,48,64]{2,1,0:T(8,128)S(1)} fusion(f32[64,48,64]{2,1,0:T(8,128)S(1)} %constant_dynamic-update-slice_fusion.109, f32[1,48,64]{2,1,0:T(8,128)S(1)} %get-tuple-element.31, pred[64]{0:T(512)(128)(4,1)S(1)} %iota_compare_fusion, pred[48]{0:T(512)(128)(4,1)S(1)} %iota_compare_fusion.1, f32[]{:T(128)} %bitcast.7, ...), kind=kLoop, calls=%fused_computation.228 | loop fusion | flops 411648 | bytes 100604
  655.9 13.6 %constant_dynamic-update-slice_fusion.107 = f32[64,48,64]{2,1,0:T(8,128)S(1)} fusion(f32[64,48,64]{2,1,0:T(8,128)S(1)} %constant_dynamic-update-slice_fusion.108, f32[1,48,64]{2,1,0:T(8,128)S(1)} %get-tuple-element.13, f32[]{:T(128)S(6)} %neg.209, pred[64]{0:T(512)(128)(4,1)S(1)} %iota_compare_fusion, pred[48]{0:T(512)(128)(4,1)S(1)} %iota_compare_fusion.1, ...), kind=kLoop, calls=%fused_computation.227 | loop fusion | flops 405504 | bytes 100604
  669.5 14.9 %constant_dynamic-update-slice_fusion.105 = f32[64,48,64]{2,1,0:T(8,128)S(1)} fusion(f32[64,48,64]{2,1,0:T(8,128)S(1)} %constant_dynamic-update-slice_fusion.106, f32[1,48,64]{2,1,0:T(8,128)S(1)} %get-tuple-element.14, f32[]{:T(128)S(6)} %neg.211, f32[]{:T(128)S(6)} %neg.210, f32[]{:T(128)} %bitcast.71, f32[]{:T(128)} %bitcast.74, f32[]{:T(128)} %bitcast.73, ...), kind=kLoop, calls=%fused_computation.225 | loop fusion | flops 442368 | bytes 100628
  685.1 3.2 constant_dynamic-update-slice_fusion.37
  688.3 3.2 constant_dynamic-update-slice_fusion.36
  691.6 3.2 constant_dynamic-update-slice_fusion.35
  694.8 2.0 constant_dynamic-update-slice_fusion.33
  696.8 2.0 constant_dynamic-update-slice_fusion.32
  706.5 3.2 constant_dynamic-update-slice_fusion.101
  709.7 3.2 constant_dynamic-update-slice_fusion.100
  712.9 3.2 constant_dynamic-update-slice_fusion.99
  716.2 2.0 constant_dynamic-update-slice_fusion.97
  718.2 2.0 constant_dynamic-update-slice_fusion.96
  729.8 2.0 constant_dynamic-update-slice_fusion.85
  741.7 2.0 constant_dynamic-update-slice_fusion.11
  743.7 2.0 constant_dynamic-update-slice_fusion.10
  745.8 2.0 constant_dynamic-update-slice_fusion.9
  753.6 3.1 constant_dynamic-update-slice_fusion.3
  756.8 4.5 constant_dynamic-update-slice_fusion.1
  761.3 4.5 constant_dynamic-update-slice_fusion
  773.4 2.0 constant_dynamic-update-slice_fusion.75
  775.4 2.0 constant_dynamic-update-slice_fusion.74
  777.4 2.0 constant_dynamic-update-slice_fusion.73
  785.3 3.1 constant_dynamic-update-slice_fusion.67
  788.5 4.5 constant_dynamic-update-slice_fusion.65
  793.0 4.5 constant_dynamic-update-slice_fusion.64
  802.4 2.7 collective-permute-done.5
  (151 shorter events, 77.5 us)
Async XLA Ops:
  2.1 57.8 %copy-start = (f32[128]{0:T(128)S(1)}, f32[128]{0:T(128)}, u32[]{:S(2)}) copy-start(f32[128]{0:T(128)} %param.3) | copy-start | bytes 1540
  42.2 102.8 %collective-permute-start = (f32[128,1,128]{0,1,2:T(1,128)S(1)}, f32[128,1,128]{0,1,2:T(1,128)S(1)}, u32[]{:S(2)}, u32[]{:S(2)}) collective-permute-start(f32[128,1,128]{0,1,2:T(1,128)S(1)} %get-tuple-element.151), channel_id=1, source_target_pairs={{0,32},{32,64},{64,96},{96,128},{128,160},{160,192},{192,224},{224... | collective-permute-start | bytes 196616 | tf_op jit(solution)/shard_map/ppermute | solution.py:22
  56.9 88.2 %collective-permute-start.1 = (f32[128,1,128]{0,1,2:T(1,128)S(1)}, f32[128,1,128]{0,1,2:T(1,128)S(1)}, u32[]{:S(2)}, u32[]{:S(2)}) collective-permute-start(f32[128,1,128]{0,1,2:T(1,128)S(1)} %get-tuple-element.152), channel_id=1, source_target_pairs={{32,0},{64,32},{96,64},{128,96},{160,128},{192,160},{224,192},{256... | collective-permute-start | bytes 196616 | tf_op jit(solution)/shard_map/ppermute | solution.py:24
  146.0 3.7 collective-permute-start.2
  146.1 3.8 collective-permute-start.3
  801.0 1.4 collective-permute-start.4
  801.0 4.0 collective-permute-start.5
  806.0 1.8 collective-permute-start.6
  806.0 3.7 collective-permute-start.7
where the time goes:
time: 826 us; the launch traced here: 811 us
  other arithmetic  582 us (70%)
  between operations  82.6 us (10%)
  blocking collectives  73.5 us (9%)
  local copies, waits for them, and re-layouts  27.9 us (3%)
  starting transfers between devices  21.9 us (3%)
  matrix products  17.1 us (2%)
    unnamed x73, other arithmetic  470 us
    div x2, other arithmetic, solve_columns(): value_im = (imag_part[level] + coef_low * value_im) / pivot  43.8 us
    div x2, other arithmetic, solve_columns(): value_re = (real_part[level] + coef_low * value_re) / pivot  43.6 us
    all_gather x1, blocking collectives, on_device(): source = lax.all_gather(residual4, 'sub', axis=2, tiled=True)  39.2 us
    all_gather x1, blocking collectives, on_device(): portion = lax.all_gather(coarse, 'grp', axis=1, tiled=True)  34.3 us
    reshape x1, local copies, waits for them, and re-layouts, on_device(): leftover.reshape(levels_z // 2, 2, rows_y // 2, 2, cols_x // 2, 2)  18.1 us
  transfers between devices with their start and end apart: 8, of which 6 were waited for; matrix products, arithmetic and copies ran while one was open for 1% of the time, Pallas kernels for 0%

commit v1 on v0

v1 whole, which is shorter than its diff:
```python
import functools
import math

import jax
import jax.numpy as jnp
from jax import lax
from jax.experimental import pallas as pl
from jax.experimental.pallas import tpu as pltpu
from jax.sharding import PartitionSpec as P

MESH = pl.DeviceIdType.MESH
HIGHEST = lax.Precision.HIGHEST
DAMPING = 0.8
LANES = 128
HALF = 64


def matmul(left, right):
    return lax.dot_general(
        left, right, (((1,), (0,)), ((), ())), precision=HIGHEST, preferred_element_type=jnp.float32
    )


def iota(shape, axis):
    return lax.broadcasted_iota(jnp.int32, shape, axis).astype(jnp.float32)


def wrapped(value, count):
    return value - count * jnp.floor((value + 0.5) * (1.0 / count))


def cos_turn(step, count):
    step = jnp.minimum(step, count - step)
    flip = step > count / 4
    step = jnp.where(flip, count / 2 - step, step)
    angle = step * (2.0 * math.pi / count)
    sq = angle * angle
    total = jnp.full_like(sq, 1.0 / math.factorial(16))
    for power in range(14, -1, -2):
        sign = 1.0 if power % 4 == 0 else -1.0
        total = total * sq + sign / math.factorial(power)
    return jnp.where(flip, -total, total)


def up_z(field):
    return pltpu.roll(field, LANES - 1, axis=field.ndim - 1)


def down_z(field):
    return pltpu.roll(field, 1, axis=field.ndim - 1)


def operate(rows, south, north, coef):
    height, upper, lower, diagonal = coef
    span = rows.shape[1]
    west = pltpu.roll(rows, 1, axis=1)
    east = pltpu.roll(rows, span - 1, axis=1)
    sides = (west + east) + (south + north)
    return diagonal * rows - height * sides - upper * up_z(rows) - lower * down_z(rows)


def kernel(
    n_grp, n_sub,
    res_ref, spacing_ref, cor_ref, coarse_ref,
    pad, table, msg1, recv1, msg2, recv2, msg3, recv3, halo, big, smooth_ref, pairs,
    scale_r, scale_p, scale_q,
    halo_send, halo_recv, send1, got1, send2, got2, send3, got3,
):
    me_g = lax.axis_index("grp")
    me_s = lax.axis_index("sub")
    ny5, nx5 = 2 * n_grp, 2 * n_sub

    def grp_at(k):
        return lax.rem(me_g + k, n_grp)

    def sub_at(k):
        return lax.rem(me_s + k, n_sub)

    ring = [(a, b) for a in (0, 1, n_grp - 1) for b in (0, 1, n_sub - 1) if (a, b) != (0, 0)]
    barrier = pltpu.get_barrier_semaphore()

    def greet_grp(k, carry):
        pl.semaphore_signal(barrier, inc=1, device_id=(grp_at(k), me_s), device_id_type=MESH)
        return carry

    def greet_sub(k, carry):
        pl.semaphore_signal(barrier, inc=1, device_id=(me_g, sub_at(k)), device_id_type=MESH)
        return carry

    lax.fori_loop(1, n_grp, greet_grp, 0)
    lax.fori_loop(1, n_sub, greet_sub, 0)
    for a, b in ring:
        if a and b:
            pl.semaphore_signal(
                barrier, inc=1, device_id=(grp_at(a), sub_at(b)), device_id_type=MESH
            )

    lane = lax.broadcasted_iota(jnp.int32, (8, LANES), 1)
    height8 = jnp.broadcast_to(spacing_ref[...], (8, LANES))
    face = 2.0 / (height8 + up_z(height8))
    upper8 = jnp.where(lane < LANES - 1, face, 0.0)
    lower8 = jnp.where(lane > 0, down_z(face), 0.0)
    diag8 = 4.0 * height8 + upper8 + lower8
    damp8 = DAMPING / diag8
    coef8 = (height8[None], upper8[None], lower8[None], diag8[None])

    pad[...] = jnp.zeros_like(pad)
    pad[2:6, 2:6, :] = res_ref[...]
    block = pad[...]
    zero_row = jnp.zeros((1, 8, LANES), jnp.float32)

    def operate_zero(rows):
        south = jnp.concatenate([zero_row, rows[:-1]], 0)
        north = jnp.concatenate([rows[1:], zero_row], 0)
        return operate(rows, south, north, coef8)

    first = damp8[None] * block
    second = first + damp8[None] * (block - operate_zero(first))
    leftover = block - operate_zero(second)
    row_pairs = jnp.concatenate([leftover[2 * j] + leftover[2 * j + 1] for j in range(4)], 0)
    z_in = lax.broadcasted_iota(jnp.int32, (LANES, LANES), 0)
    z_out = lax.broadcasted_iota(jnp.int32, (LANES, LANES), 1)
    gather_z = jnp.where((z_in >> 1) == (z_out & (HALF - 1)), 1.0, 0.0)
    pairs[...] = matmul(row_pairs, 0.25 * gather_z)
    parts = pairs[pl.ds(0, 16, stride=2), :] + pairs[pl.ds(1, 16, stride=2), :]

    shape_t = (n_grp, LANES)
    owner = lax.broadcasted_iota(jnp.int32, shape_t, 0) + me_g
    owner = jnp.where(owner >= n_grp, owner - n_grp, owner).astype(jnp.float32)
    second_half = lax.broadcasted_iota(jnp.int32, shape_t, 1) >= HALF
    alone = owner == 0.0
    wave = jnp.where(alone & second_half, 1.0 * n_grp, owner)
    shift = jnp.where(second_half & jnp.logical_not(alone), 0.25 * ny5, 0.0)
    for j in range(4):
        row = wrapped((2 * me_g + (j - 1)).astype(jnp.float32), ny5)
        table[j] = cos_turn(wrapped(wave * row - shift, ny5), ny5)

    for k in range(n_grp):
        total = table[0, k : k + 1, :] * parts[0:4]
        for j in range(1, 4):
            total = total + table[j, k : k + 1, :] * parts[4 * j : 4 * j + 4]
        if k == 0:
            recv1[0] = total
        else:
            msg1[k] = total

    pl.semaphore_wait(barrier, n_grp + n_sub - 2 + 4)

    def send_1(k, carry):
        pltpu.make_async_remote_copy(
            src_ref=msg1.at[k], dst_ref=recv1.at[k], send_sem=send1, recv_sem=got1,
            device_id=(grp_at(k), me_s), device_id_type=MESH,
        ).start()
        return carry

    lax.fori_loop(1, n_grp, send_1, 0)
    for place, (a, b) in enumerate(ring):
        pltpu.make_async_remote_copy(
            src_ref=res_ref, dst_ref=halo.at[place], send_sem=halo_send, recv_sem=halo_recv,
            device_id=(grp_at(a), sub_at(b)), device_id_type=MESH,
        ).start()

    lane_m = lax.broadcasted_iota(jnp.int32, (nx5, LANES), 1)
    row_m = lax.broadcasted_iota(jnp.int32, (nx5, LANES), 0)
    z5 = lane_m & (HALF - 1)
    height5 = matmul(height8, gather_z)
    face5 = 2.0 / (height5 + up_z(height5))
    z5_8 = lane & (HALF - 1)
    upper5 = jnp.where(z5_8 < HALF - 1, face5, 0.0)[0:1]
    lower5 = jnp.where(z5_8 > 0, down_z(face5), 0.0)[0:1]
    height5 = height5[0:1]
    mode = row_m.astype(jnp.float32)
    wave_x = jnp.where(mode > n_sub, mode - n_sub, mode)
    sin_x = cos_turn(n_sub - wave_x, 2 * nx5)
    me_gf = me_g.astype(jnp.float32)
    half_m = lane_m >= HALF
    wave_y = jnp.where(half_m, jnp.where(me_gf == 0.0, 1.0 * n_grp, me_gf), me_gf)
    sin_y = cos_turn(n_grp - wave_y, 2 * ny5)
    lam = sin_x * sin_x + sin_y * sin_y
    still = (row_m == 0) & (wave_y == 0.0)
    anchor = jnp.where(still & (z5 == 0), 1.0, 0.0)
    excess = lam * height5 + anchor
    inverse = 1.0 / (excess + upper5 + lower5)
    below = lower5 * inverse
    above = upper5 * inverse
    excess = excess * inverse
    first_scale = inverse
    weight = jnp.where(me_gf == 0.0, 1.0 / ny5, 2.0 / ny5)
    for level in range(6):
        step = 1 << level
        below_dn = pltpu.roll(below, step, axis=1)
        above_up = pltpu.roll(above, LANES - step, axis=1)
        excess_dn = pltpu.roll(excess, step, axis=1)
        excess_up = pltpu.roll(excess, LANES - step, axis=1)
        inverse = 1.0 / (excess + below * (below_dn + excess_dn) + above * (above_up + excess_up))
        low, high = below * inverse, above * inverse
        last = weight if level == 5 else 1.0
        scale_r[level] = inverse * last
        scale_p[level] = low * last
        scale_q[level] = high * last
        excess = excess * inverse + low * excess_dn + high * excess_up
        below, above = low * below_dn, high * above_up

    shape_f = (nx5, 4 * n_sub)
    mode_f, col_f = iota(shape_f, 0), iota(shape_f, 1)
    place_f = jnp.floor((col_f + 0.5) * 0.25)
    column_f = wrapped(2.0 * place_f + (col_f - 4.0 * place_f) - 1.0, nx5)
    odd_f = mode_f > n_sub
    phase_f = jnp.where(odd_f, mode_f - n_sub, mode_f) * column_f - jnp.where(odd_f, 0.25 * nx5, 0.0)
    forward_x = cos_turn(wrapped(phase_f, nx5), nx5)
    shape_b = (8, nx5)
    mode_b, col_b = iota(shape_b, 1), iota(shape_b, 0) - 1.0
    odd_b = mode_b > n_sub
    phase_b = jnp.where(odd_b, mode_b - n_sub, mode_b) * col_b - jnp.where(odd_b, 0.25 * nx5, 0.0)
    once = (mode_b == 0.0) | (mode_b == 1.0 * n_sub)
    backward_x = cos_turn(wrapped(phase_b, nx5), nx5) * jnp.where(once, 1.0 / nx5, 2.0 / nx5)

    pltpu.make_async_copy(recv1.at[pl.ds(1, n_grp - 1)], recv1.at[pl.ds(1, n_grp - 1)], got1).wait()
    own = jnp.sum(recv1[...], axis=0)
    msg2[...] = own
    recv2[0] = own

    def send_2(k, carry):
        pltpu.make_async_remote_copy(
            src_ref=msg2, dst_ref=recv2.at[n_sub - k], send_sem=send2, recv_sem=got2,
            device_id=(me_g, sub_at(k)), device_id_type=MESH,
        ).start()
        return carry

    lax.fori_loop(1, n_sub, send_2, 0)
    pltpu.make_async_copy(recv2.at[pl.ds(1, n_sub - 1)], recv2.at[pl.ds(1, n_sub - 1)], got2).wait()

    rows_in = jnp.concatenate([recv2[k] for k in range(n_sub)], 0)
    field = matmul(forward_x, rows_in)
    mean = jnp.sum(jnp.where(still, field, 0.0)) * (1.0 / HALF)
    field = jnp.where(still, field - mean, field) * first_scale
    for level in range(6):
        step = 1 << level
        field = (
            scale_r[level] * field
            + scale_p[level] * pltpu.roll(field, step, axis=1)
            + scale_q[level] * pltpu.roll(field, LANES - step, axis=1)
        )
    back = matmul(backward_x, field)[0:4]
    msg3[...] = back
    recv3[0] = back

    def send_3(k, carry):
        pltpu.make_async_remote_copy(
            src_ref=msg3, dst_ref=recv3.at[n_grp - k], send_sem=send3, recv_sem=got3,
            device_id=(grp_at(k), me_s), device_id_type=MESH,
        ).start()
        return carry

    lax.fori_loop(1, n_grp, send_3, 0)

    pltpu.make_async_copy(halo, halo, halo_recv).wait()
    big[:, 12:16, :] = jnp.zeros((12, 4, LANES), jnp.float32)
    big[4:8, 4:8, :] = res_ref[...]
    for place, (a, b) in enumerate(ring):
        at_y = {0: 4, 1: 0, n_grp - 1: 8}[a]
        at_x = {0: 4, 1: 0, n_sub - 1: 8}[b]
        big[at_y : at_y + 4, at_x : at_x + 4, :] = halo[place]
    wide = big[...]
    coef1 = tuple(value[:, 0:1] for value in coef8)
    damp1 = damp8[None, 0:1]
    first_w = damp1 * wide
    inner = first_w[1:-1] + damp1 * (
        wide[1:-1] - operate(first_w[1:-1], first_w[:-2], first_w[2:], coef1)
    )
    smooth_ref[...] = inner[1:-1]
    smooth = smooth_ref[:, 2:10, :]
    near = big[2:10, 2:10, :]

    pltpu.make_async_copy(recv3.at[pl.ds(1, n_grp - 1)], recv3.at[pl.ds(1, n_grp - 1)], got3).wait()
    for j in range(4):
        total = table[j, 0:1, :] * recv3[0]
        for k in range(1, n_grp):
            total = total + table[j, k : k + 1, :] * recv3[k]
        if j in (1, 2):
            folded = total + pltpu.roll(total, HALF, axis=1)
            coarse_ref[j - 1] = folded[1:3, 0:HALF]
        pairs[pl.ds(8 * j, 4, stride=2), :] = total
        pairs[pl.ds(8 * j + 1, 4, stride=2), :] = total
    spread_z = jnp.where((z_out >> 1) == (z_in & (HALF - 1)), 1.0, 0.0)
    coarse = matmul(pairs[...], spread_z)
    lifted = smooth + jnp.concatenate(
        [coarse[8 * (j // 2) : 8 * (j // 2) + 8][None] for j in range(8)], 0
    )
    lifted = lifted[1:-1] + damp8[None] * (
        near[1:-1] - operate(lifted[1:-1], lifted[:-2], lifted[2:], coef8)
    )
    lifted = lifted[1:-1] + damp8[None] * (
        near[2:-2] - operate(lifted[1:-1], lifted[:-2], lifted[2:], coef8)
    )
    cor_ref[...] = lifted[:, 2:6, :]

    pltpu.make_async_copy(halo, halo, halo_send).wait()
    pltpu.make_async_copy(recv1.at[pl.ds(1, n_grp - 1)], recv1.at[pl.ds(1, n_grp - 1)], send1).wait()
    pltpu.make_async_copy(recv2.at[pl.ds(1, n_sub - 1)], recv2.at[pl.ds(1, n_sub - 1)], send2).wait()
    pltpu.make_async_copy(recv3.at[pl.ds(1, n_grp - 1)], recv3.at[pl.ds(1, n_grp - 1)], send3).wait()


def on_device(n_grp, n_sub, residual4, spacing):
    f32 = jnp.float32
    nx5 = 2 * n_sub
    dma = pltpu.SemaphoreType.DMA
    vmem = pl.BlockSpec(memory_space=pltpu.VMEM)
    correction, coarse = pl.pallas_call(
        functools.partial(kernel, n_grp, n_sub),
        out_shape=(
            jax.ShapeDtypeStruct((4, 4, LANES), f32),
            jax.ShapeDtypeStruct((2, 2, HALF), f32),
        ),
        in_specs=[vmem, vmem],
        out_specs=(vmem, vmem),
        scratch_shapes=[
            pltpu.VMEM((8, 8, LANES), f32),
            pltpu.VMEM((4, n_grp, LANES), f32),
            pltpu.VMEM((n_grp, 4, LANES), f32),
            pltpu.VMEM((n_grp, 4, LANES), f32),
            pltpu.VMEM((4, LANES), f32),
            pltpu.VMEM((n_sub, 4, LANES), f32),
            pltpu.VMEM((4, LANES), f32),
            pltpu.VMEM((n_grp, 4, LANES), f32),
            pltpu.VMEM((8, 4, 4, LANES), f32),
            pltpu.VMEM((12, 16, LANES), f32),
            pltpu.VMEM((8, 16, LANES), f32),
            pltpu.VMEM((32, LANES), f32),
            pltpu.VMEM((6, nx5, LANES), f32),
            pltpu.VMEM((6, nx5, LANES), f32),
            pltpu.VMEM((6, nx5, LANES), f32),
        ]
        + [dma] * 8,
        compiler_params=pltpu.CompilerParams(collective_id=0, has_side_effects=True),
    )(jnp.transpose(residual4, (1, 2, 0)), spacing.reshape(1, LANES))
    return jnp.transpose(correction, (2, 0, 1)), jnp.transpose(coarse, (2, 0, 1))


def solution(mesh):
    placed = P(None, "grp", "sub")
    return jax.shard_map(
        functools.partial(on_device, mesh.shape["grp"], mesh.shape["sub"]),
        mesh=mesh,
        in_specs=(placed, P()),
        out_specs=(placed, placed),
        check_vma=False,
    )
```

time: 826 us -> 44 us (0.05); the launches traced: 811 us -> 43.8 us
  other arithmetic: 582 us -> 0 us
  between operations: 82.6 us -> 0.65 us
  blocking collectives: 73.5 us -> 0 us
  Pallas kernels: 0 us -> 41.3 us
  local copies, waits for them, and re-layouts: 27.9 us -> 1.88 us
  starting transfers between devices: 21.9 us -> 0 us
  matrix products: 17.1 us -> 0 us
    unnamed x73 -> x0, other arithmetic: 470 us -> none
    div x8 -> x0, other arithmetic: 88.4 us -> none  [the longest x2 43.8 us: solve_columns(): value_im = (imag_part[level] + coef_low * value_im) / pivot]
    all_gather x2 -> x0, blocking collectives: 73.5 us -> none  [the longest x1 39.2 us: on_device(): source = lax.all_gather(residual4, 'sub', axis=2, tiled=True)]
    pallas_call x0 -> x1, Pallas kernels: none -> 41.3 us  [on_device(): pl.pallas_call(functools.partial(kernel, n_grp, n_sub), out_shape=(jax.Sh...]
    ppermute x8 -> x0, starting transfers between devices: 21.9 us -> none  [the longest x4 14.7 us: padded(): lax.ppermute(tail, axis, [(i, (i + 1) % count) for i in range(count)])]
    reshape x3 -> x0, local copies, waits for them, and re-layouts: 18.3 us -> none  [the longest x1 18.1 us: on_device(): leftover.reshape(levels_z // 2, 2, rows_y // 2, 2, cols_x // 2, 2)]
    dot_general x12 -> x0, matrix products: 17.1 us -> none  [the longest x1 2.79 us: on_device(): jnp.einsum('zya,by->zba', along_s, cos_y, precision=highest)]
    reduce_sum x4 -> x0, other arithmetic: 9.52 us -> none  [the longest x1 7 us: on_device(): leftover.reshape(levels_z // 2, 2, rows_y // 2, 2, cols_x // 2, 2)]
  transfers between devices with their start and end apart: 8 -> 0, of which waited for: 6 -> 0; matrix products, arithmetic and copies ran while one was open for 1% -> 0% of each run, Pallas kernels for 0% -> 0%
where the time goes in v1:
time: 44 us; the launch traced here: 43.8 us
  Pallas kernels  41.3 us (94%)
  local copies, waits for them, and re-layouts  1.88 us (4%)
  between operations  0.65 us (1%)
    pallas_call x1, Pallas kernels, on_device(): pl.pallas_call(functools.partial(kernel, n_grp, n_sub), out_shape=(jax.Sh...  41.3 us
    unnamed x4, local copies, waits for them, and re-layouts  1.88 us

profile of v1, /device:TPU:1, one launch (start us, length us, event | category | flops | bytes accessed | tf_op | source)
XLA Modules:
  0.0 43.8 jit_solution(1581175607885345590)
XLA Ops:
  0.6 41.3 %shard_map.41 = (f32[4,4,128]{2,1,0:T(4,128)}, f32[2,2,64]{2,1,0:T(2,128)}) custom-call(f32[4,4,128]{2,1,0:T(4,128)} %bitcast.4, f32[1,128]{1,0:T(1,128)} %bitcast.7), custom_call_target="tpu_custom_call" | custom-call | tf_op jit(solution)/shard_map/pallas_call | solution.py:309
  41.9 0.0 copy-start
  42.0 1.3 %copy.6 = f32[128,4,4]{0,2,1:T(4,128)} copy(f32[128,4,4]{0,2,1:T(4,128)} %bitcast.5) | data formatting | bytes 16384
  43.2 0.0 copy-done
  43.2 0.6 %copy.7 = f32[64,2,2]{0,2,1:T(2,128)} copy(f32[64,2,2]{0,2,1:T(2,128)S(1)} %bitcast.6) | data formatting | bytes 2048
Async XLA Ops:
  41.9 1.3 %copy-start = (f32[2,2,64]{2,1,0:T(2,128)S(1)}, f32[2,2,64]{2,1,0:T(2,128)}, u32[]{:S(2)}) copy-start(f32[2,2,64]{2,1,0:T(2,128)} %get-tuple-element.5) | copy-start | bytes 3076

commit v2 on v1

v2 whole, which is shorter than its diff:
```python
import functools
import math

import jax
import jax.numpy as jnp
from jax import lax
from jax.experimental import pallas as pl
from jax.experimental.pallas import tpu as pltpu
from jax.sharding import PartitionSpec as P

MESH = pl.DeviceIdType.MESH
HIGHEST = lax.Precision.HIGHEST
DAMPING = 0.8
LANES = 128
HALF = 64


def matmul(left, right):
    return lax.dot_general(
        left, right, (((1,), (0,)), ((), ())), precision=HIGHEST, preferred_element_type=jnp.float32
    )


def iota(shape, axis):
    return lax.broadcasted_iota(jnp.int32, shape, axis).astype(jnp.float32)


def wrapped(value, count):
    return value - count * jnp.floor((value + 0.5) * (1.0 / count))


def cos_turn(step, count):
    step = jnp.minimum(step, count - step)
    flip = step > count / 4
    step = jnp.where(flip, count / 2 - step, step)
    angle = step * (2.0 * math.pi / count)
    sq = angle * angle
    total = jnp.full_like(sq, 1.0 / math.factorial(16))
    for power in range(14, -1, -2):
        sign = 1.0 if power % 4 == 0 else -1.0
        total = total * sq + sign / math.factorial(power)
    return jnp.where(flip, -total, total)


def up_z(field):
    return pltpu.roll(field, LANES - 1, axis=field.ndim - 1)


def down_z(field):
    return pltpu.roll(field, 1, axis=field.ndim - 1)


def operate(rows, south, north, coef):
    height, upper, lower, diagonal = coef
    span = rows.shape[1]
    west = pltpu.roll(rows, 1, axis=1)
    east = pltpu.roll(rows, span - 1, axis=1)
    sides = (west + east) + (south + north)
    return diagonal * rows - height * sides - upper * up_z(rows) - lower * down_z(rows)


def torus(n_grp, n_sub):
    inner = 8 if n_sub % 8 == 0 else 2
    return (n_grp // 2, 2), (n_sub // inner, inner)


def offsets(sizes):
    outer, inner = sizes

    def hops(step):
        return min(step[0], outer - step[0]) + min(step[1], inner - step[1])

    steps = [(a, b) for a in range(outer) for b in range(inner) if (a, b) != (0, 0)]
    return sorted(steps, key=hops, reverse=True)


def kernel(
    n_grp, n_sub,
    res_hbm, spacing_hbm, cor_ref, coarse_ref,
    res_ref, spacing_ref, pad, table, msg1, recv1, msg2, recv2, msg3, recv3, halo, big, smooth_ref,
    pairs, scale_r, scale_p, scale_q,
    load1, load2, halo_send, halo_recv, send1, got1, send2, got2, send3, got3,
):
    me_g = lax.axis_index("grp")
    me_s = lax.axis_index("sub")
    ny5, nx5 = 2 * n_grp, 2 * n_sub
    grp_size, sub_size = torus(n_grp, n_sub)

    def moved(me, step, sizes):
        outer, inner = sizes
        high, low = me // inner, me % inner
        return ((high + step[0]) % outer) * inner + (low + step[1]) % inner

    def slot(step, sizes):
        outer, inner = sizes
        return (-step[0] % outer) * inner + (-step[1] % inner)

    grp_steps, sub_steps = offsets(grp_size), offsets(sub_size)
    ring = [(a, b) for a in (0, 1, n_grp - 1) for b in (0, 1, n_sub - 1) if (a, b) != (0, 0)]

    load_res = pltpu.make_async_copy(res_hbm, res_ref, load1)
    load_spacing = pltpu.make_async_copy(spacing_hbm, spacing_ref, load2)
    load_res.start()
    load_spacing.start()
    barrier = pltpu.get_barrier_semaphore()

    def greet(device):
        pl.semaphore_signal(barrier, inc=1, device_id=device, device_id_type=MESH)

    for place in range(max(len(grp_steps), len(sub_steps))):
        if place < len(grp_steps):
            greet((moved(me_g, grp_steps[place], grp_size), me_s))
        if place < len(sub_steps):
            greet((me_g, moved(me_s, sub_steps[place], sub_size)))
    for a, b in ring:
        if a and b:
            greet(((me_g + a) % n_grp, (me_s + b) % n_sub))

    shape_t = (n_sub, LANES)
    place_t = lax.broadcasted_iota(jnp.int32, shape_t, 0)
    outer, inner = sub_size
    high = me_s // inner + lax.shift_right_logical(place_t, inner.bit_length() - 1)
    low = me_s % inner + (place_t & (inner - 1))
    high = jnp.where(high >= outer, high - outer, high)
    low = jnp.where(low >= inner, low - inner, low)
    owner = (high * inner + low).astype(jnp.float32)
    second_half = lax.broadcasted_iota(jnp.int32, shape_t, 1) >= HALF
    alone = owner == 0.0
    wave = jnp.where(alone & second_half, 1.0 * n_sub, owner)
    shift = jnp.where(second_half & jnp.logical_not(alone), 0.25 * nx5, 0.0)
    for j in range(4):
        column = wrapped((2 * me_s + (j - 1)).astype(jnp.float32), nx5)
        table[j] = cos_turn(wrapped(wave * column - shift, nx5), nx5)

    load_spacing.wait()
    lane = lax.broadcasted_iota(jnp.int32, (8, LANES), 1)
    height8 = jnp.broadcast_to(spacing_ref[...], (8, LANES))
    face = 2.0 / (height8 + up_z(height8))
    upper8 = jnp.where(lane < LANES - 1, face, 0.0)
    lower8 = jnp.where(lane > 0, down_z(face), 0.0)
    diag8 = 4.0 * height8 + upper8 + lower8
    damp8 = DAMPING / diag8
    coef8 = (height8[None], upper8[None], lower8[None], diag8[None])

    pad[...] = jnp.zeros_like(pad)
    load_res.wait()
    pad[2:6, 2:6, :] = res_ref[...]
    block = pad[...]
    zero_row = jnp.zeros((1, 8, LANES), jnp.float32)

    def operate_zero(rows):
        south = jnp.concatenate([zero_row, rows[:-1]], 0)
        north = jnp.concatenate([rows[1:], zero_row], 0)
        return operate(rows, south, north, coef8)

    first = damp8[None] * block
    second = first + damp8[None] * (block - operate_zero(first))
    leftover = block - operate_zero(second)
    row_pairs = jnp.concatenate([leftover[2 * j] + leftover[2 * j + 1] for j in range(4)], 0)
    z_in = lax.broadcasted_iota(jnp.int32, (LANES, LANES), 0)
    z_out = lax.broadcasted_iota(jnp.int32, (LANES, LANES), 1)
    gather_z = jnp.where((z_in >> 1) == (z_out & (HALF - 1)), 1.0, 0.0)
    pairs[...] = matmul(row_pairs, 0.25 * gather_z)
    parts = [
        pairs[pl.ds(2 * j, 4, stride=8), :] + pairs[pl.ds(2 * j + 1, 4, stride=8), :]
        for j in range(4)
    ]
    for k in range(n_sub):
        total = table[0, k : k + 1, :] * parts[0]
        for j in range(1, 4):
            total = total + table[j, k : k + 1, :] * parts[j]
        if k == 0:
            recv1[0] = total
        else:
            msg1[k] = total

    pl.semaphore_wait(barrier, n_grp + n_sub - 2 + 4)

    for step in sub_steps:
        pltpu.make_async_remote_copy(
            src_ref=msg1.at[step[0] * inner + step[1]], dst_ref=recv1.at[slot(step, sub_size)],
            send_sem=send1, recv_sem=got1,
            device_id=(me_g, moved(me_s, step, sub_size)), device_id_type=MESH,
        ).start()

    lane_m = lax.broadcasted_iota(jnp.int32, (ny5, LANES), 1)
    row_m = lax.broadcasted_iota(jnp.int32, (ny5, LANES), 0)
    z5 = lane_m & (HALF - 1)
    height5 = matmul(height8, gather_z)
    face5 = 2.0 / (height5 + up_z(height5))
    z5_8 = lane & (HALF - 1)
    upper5 = jnp.where(z5_8 < HALF - 1, face5, 0.0)[0:1]
    lower5 = jnp.where(z5_8 > 0, down_z(face5), 0.0)[0:1]
    height5 = height5[0:1]
    mode = row_m.astype(jnp.float32)
    wave_y = jnp.where(mode > n_grp, mode - n_grp, mode)
    sin_y = cos_turn(n_grp - wave_y, 2 * ny5)
    me_sf = me_s.astype(jnp.float32)
    wave_x = jnp.where((lane_m >= HALF) & (me_sf == 0.0), 1.0 * n_sub, me_sf)
    sin_x = cos_turn(n_sub - wave_x, 2 * nx5)
    lam = sin_x * sin_x + sin_y * sin_y
    still = (row_m == 0) & (wave_x == 0.0)
    anchor = jnp.where(still & (z5 == 0), 1.0, 0.0)
    excess = lam * height5 + anchor
    inverse = 1.0 / (excess + upper5 + lower5)
    below = lower5 * inverse
    above = upper5 * inverse
    excess = excess * inverse
    first_scale = inverse
    weight = jnp.where(me_sf == 0.0, 1.0 / nx5, 2.0 / nx5)
    for level in range(6):
        step = 1 << level
        below_dn = pltpu.roll(below, step, axis=1)
        above_up = pltpu.roll(above, LANES - step, axis=1)
        excess_dn = pltpu.roll(excess, step, axis=1)
        excess_up = pltpu.roll(excess, LANES - step, axis=1)
        inverse = 1.0 / (excess + below * (below_dn + excess_dn) + above * (above_up + excess_up))
        low, high = below * inverse, above * inverse
        last = weight if level == 5 else 1.0
        scale_r[level] = inverse * last
        scale_p[level] = low * last
        scale_q[level] = high * last
        excess = excess * inverse + low * excess_dn + high * excess_up
        below, above = low * below_dn, high * above_up

    shape_f = (ny5, 4 * n_grp)
    mode_f, col_f = iota(shape_f, 0), iota(shape_f, 1)
    place_f = jnp.floor((col_f + 0.5) * 0.25)
    pair_f = jnp.floor((place_f + 0.5) * 0.5)
    side = 1.0 - 2.0 * (me_g % 2).astype(jnp.float32)
    row_f = 4.0 * pair_f + 2.0 * side * (place_f - 2.0 * pair_f) + (col_f - 4.0 * place_f) - 1.0
    odd_f = mode_f > n_grp
    phase_f = jnp.where(odd_f, mode_f - n_grp, mode_f) * wrapped(row_f, ny5)
    phase_f = phase_f - jnp.where(odd_f, 0.25 * ny5, 0.0)
    forward_y = cos_turn(wrapped(phase_f, ny5), ny5)
    shape_b = (8, ny5)
    mode_b, row_b = iota(shape_b, 1), iota(shape_b, 0) - 1.0
    odd_b = mode_b > n_grp
    phase_b = jnp.where(odd_b, mode_b - n_grp, mode_b) * row_b - jnp.where(odd_b, 0.25 * ny5, 0.0)
    once = (mode_b == 0.0) | (mode_b == 1.0 * n_grp)
    backward_y = cos_turn(wrapped(phase_b, ny5), ny5) * jnp.where(once, 1.0 / ny5, 2.0 / ny5)

    pltpu.make_async_copy(recv1.at[pl.ds(1, n_sub - 1)], recv1.at[pl.ds(1, n_sub - 1)], got1).wait()
    own = jnp.sum(recv1[...], axis=0)
    msg2[...] = own
    recv2[0] = own
    for step in grp_steps:
        pltpu.make_async_remote_copy(
            src_ref=msg2, dst_ref=recv2.at[slot(step, grp_size)], send_sem=send2, recv_sem=got2,
            device_id=(moved(me_g, step, grp_size), me_s), device_id_type=MESH,
        ).start()
    for place, (a, b) in enumerate(ring):
        pltpu.make_async_remote_copy(
            src_ref=res_ref, dst_ref=halo.at[place], send_sem=halo_send, recv_sem=halo_recv,
            device_id=((me_g + a) % n_grp, (me_s + b) % n_sub), device_id_type=MESH,
        ).start()
    pltpu.make_async_copy(recv2.at[pl.ds(1, n_grp - 1)], recv2.at[pl.ds(1, n_grp - 1)], got2).wait()

    rows_in = jnp.concatenate([recv2[k] for k in range(n_grp)], 0)
    field = matmul(forward_y, rows_in)
    mean = jnp.sum(jnp.where(still, field, 0.0)) * (1.0 / HALF)
    field = jnp.where(still, field - mean, field) * first_scale
    for level in range(6):
        step = 1 << level
        field = (
            scale_r[level] * field
            + scale_p[level] * pltpu.roll(field, step, axis=1)
            + scale_q[level] * pltpu.roll(field, LANES - step, axis=1)
        )
    back = matmul(backward_y, field)[0:4]
    msg3[...] = back
    recv3[0] = back
    for step in sub_steps:
        pltpu.make_async_remote_copy(
            src_ref=msg3, dst_ref=recv3.at[slot(step, sub_size)], send_sem=send3, recv_sem=got3,
            device_id=(me_g, moved(me_s, step, sub_size)), device_id_type=MESH,
        ).start()

    pltpu.make_async_copy(halo, halo, halo_recv).wait()
    big[:, 12:16, :] = jnp.zeros((12, 4, LANES), jnp.float32)
    big[4:8, 4:8, :] = res_ref[...]
    for place, (a, b) in enumerate(ring):
        at_y = {0: 4, 1: 0, n_grp - 1: 8}[a]
        at_x = {0: 4, 1: 0, n_sub - 1: 8}[b]
        big[at_y : at_y + 4, at_x : at_x + 4, :] = halo[place]
    wide = big[...]
    coef1 = tuple(value[:, 0:1] for value in coef8)
    damp1 = damp8[None, 0:1]
    first_w = damp1 * wide
    inner_w = first_w[1:-1] + damp1 * (
        wide[1:-1] - operate(first_w[1:-1], first_w[:-2], first_w[2:], coef1)
    )
    smooth_ref[...] = inner_w[1:-1]
    smooth = smooth_ref[:, 2:10, :]
    near = big[2:10, 2:10, :]

    pltpu.make_async_copy(recv3.at[pl.ds(1, n_sub - 1)], recv3.at[pl.ds(1, n_sub - 1)], got3).wait()
    for j in range(4):
        total = table[j, 0:1, :] * recv3[0]
        for k in range(1, n_sub):
            total = total + table[j, k : k + 1, :] * recv3[k]
        pairs[pl.ds(2 * j, 4, stride=8), :] = total
        pairs[pl.ds(2 * j + 1, 4, stride=8), :] = total
    for j in (1, 2):
        both = pairs[pl.ds(8 * j + 2, 2, stride=2), :]
        coarse_ref[j - 1] = (both + pltpu.roll(both, HALF, axis=1))[:, 0:HALF]
    spread_z = jnp.where((z_out >> 1) == (z_in & (HALF - 1)), 1.0, 0.0)
    coarse = matmul(pairs[...], spread_z)
    lifted = smooth + jnp.concatenate(
        [coarse[8 * (j // 2) : 8 * (j // 2) + 8][None] for j in range(8)], 0
    )
    lifted = lifted[1:-1] + damp8[None] * (
        near[1:-1] - operate(lifted[1:-1], lifted[:-2], lifted[2:], coef8)
    )
    lifted = lifted[1:-1] + damp8[None] * (
        near[2:-2] - operate(lifted[1:-1], lifted[:-2], lifted[2:], coef8)
    )
    cor_ref[...] = lifted[:, 2:6, :]

    pltpu.make_async_copy(halo, halo, halo_send).wait()
    pltpu.make_async_copy(recv1.at[pl.ds(1, n_sub - 1)], recv1.at[pl.ds(1, n_sub - 1)], send1).wait()
    pltpu.make_async_copy(recv2.at[pl.ds(1, n_grp - 1)], recv2.at[pl.ds(1, n_grp - 1)], send2).wait()
    pltpu.make_async_copy(recv3.at[pl.ds(1, n_sub - 1)], recv3.at[pl.ds(1, n_sub - 1)], send3).wait()


def on_device(n_grp, n_sub, residual4, spacing):
    f32 = jnp.float32
    ny5 = 2 * n_grp
    dma = pltpu.SemaphoreType.DMA
    vmem = pl.BlockSpec(memory_space=pltpu.VMEM)
    anywhere = pl.BlockSpec(memory_space=pl.ANY)
    correction, coarse = pl.pallas_call(
        functools.partial(kernel, n_grp, n_sub),
        out_shape=(
            jax.ShapeDtypeStruct((4, 4, LANES), f32),
            jax.ShapeDtypeStruct((2, 2, HALF), f32),
        ),
        in_specs=[anywhere, anywhere],
        out_specs=(vmem, vmem),
        scratch_shapes=[
            pltpu.VMEM((4, 4, LANES), f32),
            pltpu.VMEM((1, LANES), f32),
            pltpu.VMEM((8, 8, LANES), f32),
            pltpu.VMEM((4, n_sub, LANES), f32),
            pltpu.VMEM((n_sub, 4, LANES), f32),
            pltpu.VMEM((n_sub, 4, LANES), f32),
            pltpu.VMEM((4, LANES), f32),
            pltpu.VMEM((n_grp, 4, LANES), f32),
            pltpu.VMEM((4, LANES), f32),
            pltpu.VMEM((n_sub, 4, LANES), f32),
            pltpu.VMEM((8, 4, 4, LANES), f32),
            pltpu.VMEM((12, 16, LANES), f32),
            pltpu.VMEM((8, 16, LANES), f32),
            pltpu.VMEM((32, LANES), f32),
            pltpu.VMEM((6, ny5, LANES), f32),
            pltpu.VMEM((6, ny5, LANES), f32),
            pltpu.VMEM((6, ny5, LANES), f32),
        ]
        + [dma] * 10,
        compiler_params=pltpu.CompilerParams(collective_id=0, has_side_effects=True),
    )(jnp.transpose(residual4, (1, 2, 0)), spacing.reshape(1, LANES))
    return jnp.transpose(correction, (2, 0, 1)), jnp.transpose(coarse, (2, 0, 1))


def solution(mesh):
    placed = P(None, "grp", "sub")
    return jax.shard_map(
        functools.partial(on_device, mesh.shape["grp"], mesh.shape["sub"]),
        mesh=mesh,
        in_specs=(placed, P()),
        out_specs=(placed, placed),
        check_vma=False,
    )
```

time: 44 us -> 41.3 us (0.939)
  Pallas kernels: 41.3 us -> 38.6 us
    pallas_call x1, Pallas kernels: 41.3 us -> 38.6 us  [on_device(): pl.pallas_call(functools.partial(kernel, n_grp, n_sub), out_shape=(jax.Sh...]
where the time goes in v2:
time: 41.3 us; the launch traced here: 41.1 us
  Pallas kernels  38.6 us (93%)
  local copies, waits for them, and re-layouts  1.88 us (5%)
  between operations  0.65 us (2%)
    pallas_call x1, Pallas kernels, on_device(): pl.pallas_call(functools.partial(kernel, n_grp, n_sub), out_shape=(jax.Sh...  38.6 us
    unnamed x4, local copies, waits for them, and re-layouts  1.88 us

profile of v2, /device:TPU:1, one launch (start us, length us, event | category | flops | bytes accessed | tf_op | source)
XLA Modules:
  0.0 41.1 jit_solution(14942288163629829571)
XLA Ops:
  0.6 38.6 %shard_map.41 = (f32[4,4,128]{2,1,0:T(4,128)}, f32[2,2,64]{2,1,0:T(2,128)}) custom-call(f32[4,4,128]{2,1,0:T(4,128)} %bitcast.4, f32[1,128]{1,0:T(1,128)} %bitcast.7), custom_call_target="tpu_custom_call" | custom-call | tf_op jit(solution)/shard_map/pallas_call | solution.py:332
  39.2 0.0 copy-start
  39.2 1.3 %copy.6 = f32[128,4,4]{0,2,1:T(4,128)} copy(f32[128,4,4]{0,2,1:T(4,128)} %bitcast.5) | data formatting | bytes 16384
  40.5 0.0 copy-done
  40.5 0.6 %copy.7 = f32[64,2,2]{0,2,1:T(2,128)} copy(f32[64,2,2]{0,2,1:T(2,128)S(1)} %bitcast.6) | data formatting | bytes 2048
Async XLA Ops:
  39.2 1.3 %copy-start = (f32[2,2,64]{2,1,0:T(2,128)S(1)}, f32[2,2,64]{2,1,0:T(2,128)}, u32[]{:S(2)}) copy-start(f32[2,2,64]{2,1,0:T(2,128)} %get-tuple-element.5) | copy-start | bytes 3076

commit v3 on v2

--- a/solution.py
+++ b/solution.py
@@ -323,6 +323,15 @@
     pltpu.make_async_copy(recv3.at[pl.ds(1, n_sub - 1)], recv3.at[pl.ds(1, n_sub - 1)], send3).wait()
 
 
+def hand_over(cor_in, coarse_in, cor_out, coarse_out, sem1, sem2):
+    first = pltpu.make_async_copy(cor_in, cor_out, sem1)
+    second = pltpu.make_async_copy(coarse_in, coarse_out, sem2)
+    first.start()
+    second.start()
+    first.wait()
+    second.wait()
+
+
 def on_device(n_grp, n_sub, residual4, spacing):
     f32 = jnp.float32
     ny5 = 2 * n_grp
@@ -332,8 +341,8 @@
     correction, coarse = pl.pallas_call(
         functools.partial(kernel, n_grp, n_sub),
         out_shape=(
-            jax.ShapeDtypeStruct((4, 4, LANES), f32),
-            jax.ShapeDtypeStruct((2, 2, HALF), f32),
+            pltpu.VMEM((4, 4, LANES), f32),
+            pltpu.VMEM((2, 2, HALF), f32),
         ),
         in_specs=[anywhere, anywhere],
         out_specs=(vmem, vmem),
@@ -359,6 +368,19 @@
         + [dma] * 10,
         compiler_params=pltpu.CompilerParams(collective_id=0, has_side_effects=True),
     )(jnp.transpose(residual4, (1, 2, 0)), spacing.reshape(1, LANES))
+    correction, coarse = pl.pallas_call(
+        hand_over,
+        out_shape=(
+            jax.ShapeDtypeStruct((4, 4, LANES), f32),
+            jax.ShapeDtypeStruct((2, 2, HALF), f32),
+        ),
+        in_specs=[vmem, vmem],
+        out_specs=(anywhere, anywhere),
+        scratch_shapes=[dma] * 2,
+    )(
+        pltpu.with_memory_space_constraint(correction, pltpu.VMEM),
+        pltpu.with_memory_space_constraint(coarse, pltpu.VMEM),
+    )
     return jnp.transpose(correction, (2, 0, 1)), jnp.transpose(coarse, (2, 0, 1))
 
 

time: 41.3 us -> 39.4 us (0.954)
  local copies, waits for them, and re-layouts: 1.88 us -> 0 us
    unnamed x4 -> x0, local copies, waits for them, and re-layouts: 1.88 us -> none
    pallas_call x1 -> x2, Pallas kernels: 38.6 us -> 38.6 us  [the longest x1 38 us: on_device(): pl.pallas_call(functools.partial(kernel, n_grp, n_sub), out_shape=(pltpu....]
where the time goes in v3:
time: 39.4 us; the launch traced here: 39.2 us
  Pallas kernels  38.6 us (98%)
  between operations  0.64 us (2%)
    pallas_call x1, Pallas kernels, on_device(): pl.pallas_call(functools.partial(kernel, n_grp, n_sub), out_shape=(pltpu....  38 us

profile of v3, /device:TPU:1, one launch (start us, length us, event | category | flops | bytes accessed | tf_op | source)
XLA Modules:
  0.0 39.2 jit_solution(7793014359670378729)
XLA Ops:
  0.6 38.0 %shard_map.41 = (f32[4,4,128]{2,1,0:T(4,128)S(1)}, f32[2,2,64]{2,1,0:T(2,128)S(1)}) custom-call(f32[4,4,128]{2,1,0:T(4,128)} %bitcast.4, f32[1,128]{1,0:T(1,128)} %bitcast.5), custom_call_target="tpu_custom_call" | custom-call | tf_op jit(solution)/shard_map/pallas_call | solution.py:341
  38.6 0.6 %shard_map.42 = (f32[4,4,128]{2,1,0:T(4,128)}, f32[2,2,64]{2,1,0:T(2,128)}) custom-call(f32[4,4,128]{2,1,0:T(4,128)S(1)} %get-tuple-element.6.cor_in, f32[2,2,64]{2,1,0:T(2,128)S(1)} %get-tuple-element.7.coarse_in), custom_call_target="tpu_custom_call" | custom-call | tf_op jit(solution)/shard_map/pallas_call | solution.py:371

commit v4 on v3

v4 whole, which is shorter than its diff:
```python
import functools
import math

import jax
import jax.numpy as jnp
from jax import lax
from jax.experimental import pallas as pl
from jax.experimental.pallas import tpu as pltpu
from jax.sharding import PartitionSpec as P

MESH = pl.DeviceIdType.MESH
HIGHEST = lax.Precision.HIGHEST
DAMPING = 0.8
LANES = 128
HALF = 64
REACH = 7


def matmul(left, right):
    return lax.dot_general(
        left, right, (((1,), (0,)), ((), ())), precision=HIGHEST, preferred_element_type=jnp.float32
    )


def iota(shape, axis):
    return lax.broadcasted_iota(jnp.int32, shape, axis).astype(jnp.float32)


def wrapped(value, count):
    return value - count * jnp.floor((value + 0.5) * (1.0 / count))


def cos_turn(step, count):
    step = jnp.minimum(step, count - step)
    flip = step > count / 4
    step = jnp.where(flip, count / 2 - step, step)
    angle = step * (2.0 * math.pi / count)
    sq = angle * angle
    total = jnp.full_like(sq, 1.0 / math.factorial(16))
    for power in range(14, -1, -2):
        sign = 1.0 if power % 4 == 0 else -1.0
        total = total * sq + sign / math.factorial(power)
    return jnp.where(flip, -total, total)


def up_z(field):
    return pltpu.roll(field, LANES - 1, axis=field.ndim - 1)


def down_z(field):
    return pltpu.roll(field, 1, axis=field.ndim - 1)


def operate(rows, south, north, coef):
    height, upper, lower, diagonal = coef
    span = rows.shape[1]
    west = pltpu.roll(rows, 1, axis=1)
    east = pltpu.roll(rows, span - 1, axis=1)
    sides = (west + east) + (south + north)
    return diagonal * rows - height * sides - upper * up_z(rows) - lower * down_z(rows)


def torus(n_sub):
    inner = 8 if n_sub % 8 == 0 else 2
    return n_sub // inner, inner


def ring_hops(step, size):
    return min(step % size, -step % size)


def hops(step, sizes):
    return ring_hops(step[0], sizes[0]) + ring_hops(step[1], sizes[1])


def compose(weights, keep, down, up, step):
    terms = {}
    for offset, weight in weights.items():
        for place, part in (
            (offset, keep * weight),
            (offset - step, down * pltpu.roll(weight, step, axis=1)),
            (offset + step, up * pltpu.roll(weight, LANES - step, axis=1)),
        ):
            terms[place] = terms[place] + part if place in terms else part
    return terms


def arrived(blocks, semaphore):
    pltpu.make_async_copy(blocks, blocks, semaphore).wait()


def solve_modes(n_grp, n_sub, me_s, height5, weights_z, forward_ref, backward_ref, still_ref):
    ny5, nx5 = 2 * n_grp, 2 * n_sub
    lane_m = lax.broadcasted_iota(jnp.int32, (ny5, LANES), 1)
    row_m = lax.broadcasted_iota(jnp.int32, (ny5, LANES), 0)
    z5 = lane_m & (HALF - 1)
    z5_8 = z5[0:8]
    face5 = 2.0 / (height5 + up_z(height5))
    upper5 = jnp.where(z5_8 < HALF - 1, face5, 0.0)[0:1]
    lower5 = jnp.where(z5_8 > 0, down_z(face5), 0.0)[0:1]
    height5 = height5[0:1]
    mode = row_m.astype(jnp.float32)
    odd = mode > n_grp
    wave_y = jnp.where(odd, mode - n_grp, mode)
    sin_y = cos_turn(n_grp - wave_y, 2 * ny5)
    me_sf = me_s.astype(jnp.float32)
    wave_x = jnp.where((lane_m >= HALF) & (me_sf == 0.0), 1.0 * n_sub, me_sf)
    sin_x = cos_turn(n_sub - wave_x, 2 * nx5)
    lam = sin_x * sin_x + sin_y * sin_y
    still = (row_m == 0) & (wave_x == 0.0)
    still_ref[...] = jnp.where(still, 1.0, 0.0)
    anchor = jnp.where(still & (z5 == 0), 1.0, 0.0)
    excess = lam * height5 + anchor
    inverse = 1.0 / (excess + upper5 + lower5)
    below = lower5 * inverse
    above = upper5 * inverse
    excess = excess * inverse
    weight = jnp.where(me_sf == 0.0, 1.0 / nx5, 2.0 / nx5)
    terms = {0: inverse}
    for level in range(6):
        step = 1 << level
        below_dn = pltpu.roll(below, step, axis=1)
        above_up = pltpu.roll(above, LANES - step, axis=1)
        excess_dn = pltpu.roll(excess, step, axis=1)
        excess_up = pltpu.roll(excess, LANES - step, axis=1)
        inverse = 1.0 / (excess + below * (below_dn + excess_dn) + above * (above_up + excess_up))
        low, high = below * inverse, above * inverse
        last = weight if level == 5 else 1.0
        keep, down, up = inverse * last, low * last, high * last
        terms = (
            {0: keep, -step: down, step: up} if level == 3 else compose(terms, keep, down, up, step)
        )
        if level % 3 == 2:
            for offset in range(-REACH, REACH + 1):
                weights_z[level // 3, REACH + offset] = terms[offset * (step >> 2)]
        excess = excess * inverse + low * excess_dn + high * excess_up
        below, above = low * below_dn, high * above_up

    shape_f = (ny5, 4 * n_grp)
    mode_f, col_f = iota(shape_f, 0), iota(shape_f, 1)
    chip_f = jnp.floor((col_f + 0.5) * 0.125)
    row_f = wrapped(4.0 * chip_f + (col_f - 8.0 * chip_f) - 1.0, ny5)
    odd_f = mode_f > n_grp
    phase_f = jnp.where(odd_f, mode_f - n_grp, mode_f) * row_f - jnp.where(odd_f, 0.25 * ny5, 0.0)
    forward_ref[...] = cos_turn(wrapped(phase_f, ny5), ny5)
    scale = jnp.where((wave_y == 0.0) | (wave_y == 1.0 * n_grp), 1.0 / ny5, 2.0 / ny5)
    quarter = jnp.where(odd, 0.25 * ny5, 0.0)
    for r in range(6):
        backward_ref[r] = cos_turn(wrapped(wave_y * (r - 1.0) - quarter, ny5), ny5) * scale


def kernel(
    n_grp, n_sub,
    res_hbm, spacing_hbm, cor_ref, coarse_ref,
    res_ref, spacing_ref, pad, table, msg1, recv1, msg2, recv2, msg3, recv3, halo, big, smooth_ref,
    pairs, weights_z, forward_ref, backward_ref, still_ref, spread_ref,
    load1, load2, halo_send, halo_recv, send1, got1, send2, got2, send3, got3,
):
    me_g = lax.axis_index("grp")
    me_s = lax.axis_index("sub")
    ny5, nx5 = 2 * n_grp, 2 * n_sub
    n_z = n_grp // 2
    sizes = torus(n_sub)
    outer, inner = sizes
    me_z, side = me_g // 2, me_g % 2
    owner_g, other_g = 2 * me_z + 1, 2 * me_z
    owns = side == 1

    def moved(step):
        return ((me_s // inner + step[0]) % outer) * inner + (me_s % inner + step[1]) % inner

    def slot(step):
        return (-step[0] % outer) * inner + (-step[1] % inner)

    here = [(a, b) for a in range(outer) for b in range(inner)]
    here.sort(key=lambda step: hops(step, sizes), reverse=True)
    away = [step for step in here if step != (0, 0)]
    along_z = sorted(range(1, n_z), key=lambda step: ring_hops(step, n_z), reverse=True)
    ring = [(a, b) for a in (0, 1, n_grp - 1) for b in (0, 1, n_sub - 1) if (a, b) != (0, 0)]

    load_res = pltpu.make_async_copy(res_hbm, res_ref, load1)
    load_spacing = pltpu.make_async_copy(spacing_hbm, spacing_ref, load2)
    load_res.start()
    load_spacing.start()
    barrier = pltpu.get_barrier_semaphore()

    def greet(device):
        pl.semaphore_signal(barrier, inc=1, device_id=device, device_id_type=MESH)

    @pl.when(owns)
    def _():
        queue = [(hops(step, sizes), 0, step) for step in here]
        queue += [(hops(step, sizes), 1, step) for step in away]
        queue += [(ring_hops(step, n_z), 2, step) for step in along_z]
        for _, kind, step in sorted(queue, reverse=True):
            if kind == 2:
                greet((2 * ((me_z + step) % n_z) + 1, me_s))
            else:
                greet((owner_g if kind else other_g, moved(step)))
        for b in (0, 1, n_sub - 1):
            greet(((me_g + 1) % n_grp, (me_s + b) % n_sub))

    @pl.when(jnp.logical_not(owns))
    def _():
        for step in here:
            greet((owner_g, moved(step)))
        for b in (1, n_sub - 1):
            greet((me_g, (me_s + b) % n_sub))
        for b in (0, 1, n_sub - 1):
            greet(((me_g + n_grp - 1) % n_grp, (me_s + b) % n_sub))

    shape_t = (n_sub, LANES)
    place_t = lax.broadcasted_iota(jnp.int32, shape_t, 0)
    high = me_s // inner + lax.shift_right_logical(place_t, inner.bit_length() - 1)
    low = me_s % inner + (place_t & (inner - 1))
    high = jnp.where(high >= outer, high - outer, high)
    low = jnp.where(low >= inner, low - inner, low)
    owner = (high * inner + low).astype(jnp.float32)
    second_half = lax.broadcasted_iota(jnp.int32, shape_t, 1) >= HALF
    alone = owner == 0.0
    wave = jnp.where(alone & second_half, 1.0 * n_sub, owner)
    shift = jnp.where(second_half & jnp.logical_not(alone), 0.25 * nx5, 0.0)
    for j in range(4):
        column = wrapped((2 * me_s + (j - 1)).astype(jnp.float32), nx5)
        table[j] = cos_turn(wrapped(wave * column - shift, nx5), nx5)

    load_spacing.wait()
    lane = lax.broadcasted_iota(jnp.int32, (8, LANES), 1)
    height8 = jnp.broadcast_to(spacing_ref[...], (8, LANES))
    face = 2.0 / (height8 + up_z(height8))
    upper8 = jnp.where(lane < LANES - 1, face, 0.0)
    lower8 = jnp.where(lane > 0, down_z(face), 0.0)
    diag8 = 4.0 * height8 + upper8 + lower8
    damp8 = DAMPING / diag8
    coef8 = (height8[None], upper8[None], lower8[None], diag8[None])

    pad[...] = jnp.zeros_like(pad)
    load_res.wait()
    pad[2:6, 2:6, :] = res_ref[...]
    block = pad[...]
    zero_row = jnp.zeros((1, 8, LANES), jnp.float32)

    def operate_zero(rows):
        south = jnp.concatenate([zero_row, rows[:-1]], 0)
        north = jnp.concatenate([rows[1:], zero_row], 0)
        return operate(rows, south, north, coef8)

    first = damp8[None] * block
    second = first + damp8[None] * (block - operate_zero(first))
    leftover = block - operate_zero(second)
    row_pairs = jnp.concatenate([leftover[2 * j] + leftover[2 * j + 1] for j in range(4)], 0)
    z_in = lax.broadcasted_iota(jnp.int32, (LANES, LANES), 0)
    z_out = lax.broadcasted_iota(jnp.int32, (LANES, LANES), 1)
    gather_z = jnp.where((z_in >> 1) == (z_out & (HALF - 1)), 1.0, 0.0)
    pairs[...] = matmul(row_pairs, 0.25 * gather_z)
    parts = [
        pairs[pl.ds(2 * j, 4, stride=8), :] + pairs[pl.ds(2 * j + 1, 4, stride=8), :]
        for j in range(4)
    ]
    for k in range(n_sub):
        total = table[0, k : k + 1, :] * parts[0]
        for j in range(1, 4):
            total = total + table[j, k : k + 1, :] * parts[j]
        msg1[k] = total

    spread_ref[...] = jnp.where((z_out >> 1) == (z_in & (HALF - 1)), 1.0, 0.0)

    pl.semaphore_wait(barrier, jnp.where(owns, 2 * n_sub - 1 + n_z - 1 + 3, n_sub + 5))

    for step in away:
        pltpu.make_async_remote_copy(
            src_ref=msg1.at[step[0] * inner + step[1]],
            dst_ref=recv1.at[side * n_sub + slot(step)], send_sem=send1, recv_sem=got1,
            device_id=(owner_g, moved(step)), device_id_type=MESH,
        ).start()

    @pl.when(jnp.logical_not(owns))
    def _():
        pltpu.make_async_remote_copy(
            src_ref=msg1.at[0], dst_ref=recv1.at[0], send_sem=send1, recv_sem=got1,
            device_id=(owner_g, me_s), device_id_type=MESH,
        ).start()

    for place, (a, b) in enumerate(ring):
        pltpu.make_async_remote_copy(
            src_ref=res_ref, dst_ref=halo.at[place], send_sem=halo_send, recv_sem=halo_recv,
            device_id=((me_g + a) % n_grp, (me_s + b) % n_sub), device_id_type=MESH,
        ).start()

    height5 = matmul(height8, gather_z)

    @pl.when(owns)
    def _():
        recv1[n_sub] = msg1[0]
        solve_modes(
            n_grp, n_sub, me_s, height5, weights_z, forward_ref, backward_ref, still_ref
        )
        arrived(recv1.at[pl.ds(0, 2 * n_sub - 1)], got1)
        other = jnp.sum(recv1[0:n_sub], axis=0)
        own = jnp.sum(recv1[n_sub : 2 * n_sub], axis=0)
        gap = jnp.zeros((2, LANES), jnp.float32)
        both = jnp.concatenate([other, gap, gap], 0) + jnp.concatenate([gap, own, gap], 0)
        msg2[...] = both
        recv2[0] = both
        for step in along_z:
            pltpu.make_async_remote_copy(
                src_ref=msg2, dst_ref=recv2.at[-step % n_z], send_sem=send2, recv_sem=got2,
                device_id=(2 * ((me_z + step) % n_z) + 1, me_s), device_id_type=MESH,
            ).start()
        arrived(recv2.at[pl.ds(1, n_z - 1)], got2)

        rows_in = recv2[...].reshape(8 * n_z, LANES)
        field = matmul(forward_ref[...], rows_in)
        column = jnp.sum(rows_in, axis=0, keepdims=True)
        low_half = lax.broadcasted_iota(jnp.int32, (1, LANES), 1) < HALF
        mean = jnp.sum(jnp.where(low_half, column, 0.0), axis=1, keepdims=True) * (1.0 / HALF)
        field = field - still_ref[...] * mean
        for group in range(2):
            total = weights_z[group, REACH] * field
            for offset in range(1, REACH + 1):
                step = offset << (3 * group)
                total = total + (
                    weights_z[group, REACH - offset] * pltpu.roll(field, step, axis=1)
                    + weights_z[group, REACH + offset] * pltpu.roll(field, LANES - step, axis=1)
                )
            field = total
        lines = []
        for r in range(6):
            line = backward_ref[r, 0:8] * field[0:8]
            for k in range(8, ny5, 8):
                line = line + backward_ref[r, k : k + 8] * field[k : k + 8]
            lines.append(jnp.sum(line, axis=0, keepdims=True))
        msg3[0] = jnp.concatenate(lines[0:4], 0)
        msg3[1] = jnp.concatenate(lines[2:6], 0)
        recv3[0] = msg3[1]
        for step in here:
            for core in (0, 1):
                if core == 0 or step != (0, 0):
                    pltpu.make_async_remote_copy(
                        src_ref=msg3.at[core], dst_ref=recv3.at[slot(step)],
                        send_sem=send3, recv_sem=got3,
                        device_id=(owner_g if core else other_g, moved(step)),
                        device_id_type=MESH,
                    ).start()

    arrived(halo, halo_recv)
    big[:, 12:16, :] = jnp.zeros((12, 4, LANES), jnp.float32)
    big[4:8, 4:8, :] = res_ref[...]
    for place, (a, b) in enumerate(ring):
        at_y = {0: 4, 1: 0, n_grp - 1: 8}[a]
        at_x = {0: 4, 1: 0, n_sub - 1: 8}[b]
        big[at_y : at_y + 4, at_x : at_x + 4, :] = halo[place]
    wide = big[...]
    coef1 = tuple(value[:, 0:1] for value in coef8)
    damp1 = damp8[None, 0:1]
    first_w = damp1 * wide
    inner_w = first_w[1:-1] + damp1 * (
        wide[1:-1] - operate(first_w[1:-1], first_w[:-2], first_w[2:], coef1)
    )
    smooth_ref[...] = inner_w[1:-1]
    smooth = smooth_ref[:, 2:10, :]
    near = big[2:10, 2:10, :]

    @pl.when(owns)
    def _():
        arrived(recv3.at[pl.ds(1, n_sub - 1)], got3)

    @pl.when(jnp.logical_not(owns))
    def _():
        arrived(recv3, got3)

    for j in range(4):
        total = table[j, 0:1, :] * recv3[0]
        for k in range(1, n_sub):
            total = total + table[j, k : k + 1, :] * recv3[k]
        pairs[pl.ds(2 * j, 4, stride=8), :] = total
        pairs[pl.ds(2 * j + 1, 4, stride=8), :] = total
    for j in (1, 2):
        both = pairs[pl.ds(8 * j + 2, 2, stride=2), :]
        coarse_ref[j - 1] = (both + pltpu.roll(both, HALF, axis=1))[:, 0:HALF]
    coarse = matmul(pairs[...], spread_ref[...])
    lifted = smooth + jnp.concatenate(
        [coarse[8 * (j // 2) : 8 * (j // 2) + 8][None] for j in range(8)], 0
    )
    lifted = lifted[1:-1] + damp8[None] * (
        near[1:-1] - operate(lifted[1:-1], lifted[:-2], lifted[2:], coef8)
    )
    lifted = lifted[1:-1] + damp8[None] * (
        near[2:-2] - operate(lifted[1:-1], lifted[:-2], lifted[2:], coef8)
    )
    cor_ref[...] = lifted[:, 2:6, :]

    arrived(halo, halo_send)

    @pl.when(owns)
    def _():
        arrived(recv1.at[pl.ds(0, n_sub - 1)], send1)
        arrived(recv2.at[pl.ds(1, n_z - 1)], send2)
        arrived(recv1.at[pl.ds(0, 2 * n_sub - 1)], send3)

    @pl.when(jnp.logical_not(owns))
    def _():
        arrived(recv1.at[pl.ds(0, n_sub)], send1)


def hand_over(cor_in, coarse_in, cor_out, coarse_out, sem1, sem2):
    first = pltpu.make_async_copy(cor_in, cor_out, sem1)
    second = pltpu.make_async_copy(coarse_in, coarse_out, sem2)
    first.start()
    second.start()
    first.wait()
    second.wait()


def on_device(n_grp, n_sub, residual4, spacing):
    f32 = jnp.float32
    ny5 = 2 * n_grp
    dma = pltpu.SemaphoreType.DMA
    vmem = pl.BlockSpec(memory_space=pltpu.VMEM)
    anywhere = pl.BlockSpec(memory_space=pl.ANY)
    correction, coarse = pl.pallas_call(
        functools.partial(kernel, n_grp, n_sub),
        out_shape=(
            pltpu.VMEM((4, 4, LANES), f32),
            pltpu.VMEM((2, 2, HALF), f32),
        ),
        in_specs=[anywhere, anywhere],
        out_specs=(vmem, vmem),
        scratch_shapes=[
            pltpu.VMEM((4, 4, LANES), f32),
            pltpu.VMEM((1, LANES), f32),
            pltpu.VMEM((8, 8, LANES), f32),
            pltpu.VMEM((4, n_sub, LANES), f32),
            pltpu.VMEM((n_sub, 4, LANES), f32),
            pltpu.VMEM((2 * n_sub, 4, LANES), f32),
            pltpu.VMEM((8, LANES), f32),
            pltpu.VMEM((n_grp // 2, 8, LANES), f32),
            pltpu.VMEM((2, 4, LANES), f32),
            pltpu.VMEM((n_sub, 4, LANES), f32),
            pltpu.VMEM((8, 4, 4, LANES), f32),
            pltpu.VMEM((12, 16, LANES), f32),
            pltpu.VMEM((8, 16, LANES), f32),
            pltpu.VMEM((32, LANES), f32),
            pltpu.VMEM((2, 2 * REACH + 1, ny5, LANES), f32),
            pltpu.VMEM((ny5, 4 * n_grp), f32),
            pltpu.VMEM((6, ny5, LANES), f32),
            pltpu.VMEM((ny5, LANES), f32),
            pltpu.VMEM((LANES, LANES), f32),
        ]
        + [dma] * 10,
        compiler_params=pltpu.CompilerParams(collective_id=0, has_side_effects=True),
    )(jnp.transpose(residual4, (1, 2, 0)), spacing.reshape(1, LANES))
    correction, coarse = pl.pallas_call(
        hand_over,
        out_shape=(
            jax.ShapeDtypeStruct((4, 4, LANES), f32),
            jax.ShapeDtypeStruct((2, 2, HALF), f32),
        ),
        in_specs=[vmem, vmem],
        out_specs=(anywhere, anywhere),
        scratch_shapes=[dma] * 2,
    )(
        pltpu.with_memory_space_constraint(correction, pltpu.VMEM),
        pltpu.with_memory_space_constraint(coarse, pltpu.VMEM),
    )
    return jnp.transpose(correction, (2, 0, 1)), jnp.transpose(coarse, (2, 0, 1))


def solution(mesh):
    placed = P(None, "grp", "sub")
    return jax.shard_map(
        functools.partial(on_device, mesh.shape["grp"], mesh.shape["sub"]),
        mesh=mesh,
        in_specs=(placed, P()),
        out_specs=(placed, placed),
        check_vma=False,
    )
```

time: 39.4 us -> 37.5 us (0.952)
  Pallas kernels: 38.6 us -> 36.7 us
    pallas_call x1, Pallas kernels: 38 us -> 36 us  [on_device(): pl.pallas_call(functools.partial(kernel, n_grp, n_sub), out_shape=(pltpu....]
where the time goes in v4:
time: 37.5 us; the launch traced here: 37.3 us
  Pallas kernels  36.7 us (98%)
  between operations  0.64 us (2%)
    pallas_call x1, Pallas kernels, on_device(): pl.pallas_call(functools.partial(kernel, n_grp, n_sub), out_shape=(pltpu....  36 us

profile of v4, /device:TPU:1, one launch (start us, length us, event | category | flops | bytes accessed | tf_op | source)
XLA Modules:
  0.0 37.3 jit_solution(11451097399479382776)
XLA Ops:
  0.6 36.0 %shard_map.41 = (f32[4,4,128]{2,1,0:T(4,128)S(1)}, f32[2,2,64]{2,1,0:T(2,128)S(1)}) custom-call(f32[4,4,128]{2,1,0:T(4,128)} %bitcast.4, f32[1,128]{1,0:T(1,128)} %bitcast.5), custom_call_target="tpu_custom_call" | custom-call | tf_op jit(solution)/shard_map/pallas_call | solution.py:421
  36.7 0.6 %shard_map.42 = (f32[4,4,128]{2,1,0:T(4,128)}, f32[2,2,64]{2,1,0:T(2,128)}) custom-call(f32[4,4,128]{2,1,0:T(4,128)S(1)} %get-tuple-element.6.cor_in, f32[2,2,64]{2,1,0:T(2,128)S(1)} %get-tuple-element.7.coarse_in), custom_call_target="tpu_custom_call" | custom-call | tf_op jit(solution)/shard_map/pallas_call | solution.py:453

commit v5 on v4

--- a/solution.py
+++ b/solution.py
@@ -85,11 +85,21 @@
     return terms
 
 
+def owner_places(n_sub):
+    outer, inner = torus(n_sub)
+
+    def rank(place):
+        step = (place // inner, place % inner)
+        return hops(step, (outer, inner)), step[1]
+
+    return sorted(range(n_sub), key=rank)[: n_sub // 2]
+
+
 def arrived(blocks, semaphore):
     pltpu.make_async_copy(blocks, blocks, semaphore).wait()
 
 
-def solve_modes(n_grp, n_sub, me_s, height5, weights_z, forward_ref, backward_ref, still_ref):
+def solve_modes(n_grp, n_sub, wave_f, height5, weights_z, still_ref):
     ny5, nx5 = 2 * n_grp, 2 * n_sub
     lane_m = lax.broadcasted_iota(jnp.int32, (ny5, LANES), 1)
     row_m = lax.broadcasted_iota(jnp.int32, (ny5, LANES), 0)
@@ -103,8 +113,7 @@
     odd = mode > n_grp
     wave_y = jnp.where(odd, mode - n_grp, mode)
     sin_y = cos_turn(n_grp - wave_y, 2 * ny5)
-    me_sf = me_s.astype(jnp.float32)
-    wave_x = jnp.where((lane_m >= HALF) & (me_sf == 0.0), 1.0 * n_sub, me_sf)
+    wave_x = jnp.where((lane_m >= HALF) & (wave_f == 0.0), 1.0 * n_sub, wave_f)
     sin_x = cos_turn(n_sub - wave_x, 2 * nx5)
     lam = sin_x * sin_x + sin_y * sin_y
     still = (row_m == 0) & (wave_x == 0.0)
@@ -115,7 +124,7 @@
     below = lower5 * inverse
     above = upper5 * inverse
     excess = excess * inverse
-    weight = jnp.where(me_sf == 0.0, 1.0 / nx5, 2.0 / nx5)
+    weight = jnp.where(wave_f == 0.0, 1.0 / nx5, 2.0 / nx5)
     terms = {0: inverse}
     for level in range(6):
         step = 1 << level
@@ -136,6 +145,12 @@
         excess = excess * inverse + low * excess_dn + high * excess_up
         below, above = low * below_dn, high * above_up
 
+
+def transforms(n_grp, forward_ref, backward_ref):
+    ny5 = 2 * n_grp
+    mode = iota((ny5, LANES), 0)
+    odd = mode > n_grp
+    wave_y = jnp.where(odd, mode - n_grp, mode)
     shape_f = (ny5, 4 * n_grp)
     mode_f, col_f = iota(shape_f, 0), iota(shape_f, 1)
     chip_f = jnp.floor((col_f + 0.5) * 0.125)
@@ -152,7 +167,7 @@
 def kernel(
     n_grp, n_sub,
     res_hbm, spacing_hbm, cor_ref, coarse_ref,
-    res_ref, spacing_ref, pad, table, msg1, recv1, msg2, recv2, msg3, recv3, halo, big, smooth_ref,
+    res_ref, spacing_ref, pad, table, table8, msg1, recv1, msg2, recv2, msg3, recv3, halo, big, smooth_ref,
     pairs, weights_z, forward_ref, backward_ref, still_ref, spread_ref,
     load1, load2, halo_send, halo_recv, send1, got1, send2, got2, send3, got3,
 ):
@@ -164,17 +179,18 @@
     outer, inner = sizes
     me_z, side = me_g // 2, me_g % 2
     owner_g, other_g = 2 * me_z + 1, 2 * me_z
-    owns = side == 1
 
     def moved(step):
         return ((me_s // inner + step[0]) % outer) * inner + (me_s % inner + step[1]) % inner
 
-    def slot(step):
-        return (-step[0] % outer) * inner + (-step[1] % inner)
+    places = owner_places(n_sub)
+    n_own = len(places)
+    own_index = sum(jnp.where(me_s == place, number, 0) for number, place in enumerate(places))
+    chosen = sum(jnp.where(me_s == place, 1, 0) for place in places)
+    owns = side * chosen == 1
 
     here = [(a, b) for a in range(outer) for b in range(inner)]
     here.sort(key=lambda step: hops(step, sizes), reverse=True)
-    away = [step for step in here if step != (0, 0)]
     along_z = sorted(range(1, n_z), key=lambda step: ring_hops(step, n_z), reverse=True)
     ring = [(a, b) for a in (0, 1, n_grp - 1) for b in (0, 1, n_sub - 1) if (a, b) != (0, 0)]
 
@@ -190,32 +206,24 @@
     @pl.when(owns)
     def _():
         queue = [(hops(step, sizes), 0, step) for step in here]
-        queue += [(hops(step, sizes), 1, step) for step in away]
+        queue += [(hops(step, sizes), 1, step) for step in here if step != (0, 0)]
         queue += [(ring_hops(step, n_z), 2, step) for step in along_z]
         for _, kind, step in sorted(queue, reverse=True):
             if kind == 2:
                 greet((2 * ((me_z + step) % n_z) + 1, me_s))
             else:
                 greet((owner_g if kind else other_g, moved(step)))
-        for b in (0, 1, n_sub - 1):
-            greet(((me_g + 1) % n_grp, (me_s + b) % n_sub))
 
     @pl.when(jnp.logical_not(owns))
     def _():
-        for step in here:
-            greet((owner_g, moved(step)))
-        for b in (1, n_sub - 1):
-            greet((me_g, (me_s + b) % n_sub))
-        for b in (0, 1, n_sub - 1):
-            greet(((me_g + n_grp - 1) % n_grp, (me_s + b) % n_sub))
+        for place in places:
+            greet((owner_g, place))
+
+    for a, b in ring:
+        greet(((me_g + a) % n_grp, (me_s + b) % n_sub))
 
     shape_t = (n_sub, LANES)
-    place_t = lax.broadcasted_iota(jnp.int32, shape_t, 0)
-    high = me_s // inner + lax.shift_right_logical(place_t, inner.bit_length() - 1)
-    low = me_s % inner + (place_t & (inner - 1))
-    high = jnp.where(high >= outer, high - outer, high)
-    low = jnp.where(low >= inner, low - inner, low)
-    owner = (high * inner + low).astype(jnp.float32)
+    owner = iota(shape_t, 0)
     second_half = lax.broadcasted_iota(jnp.int32, shape_t, 1) >= HALF
     alone = owner == 0.0
     wave = jnp.where(alone & second_half, 1.0 * n_sub, owner)
@@ -261,25 +269,21 @@
         total = table[0, k : k + 1, :] * parts[0]
         for j in range(1, 4):
             total = total + table[j, k : k + 1, :] * parts[j]
-        msg1[k] = total
+        msg1[k // 2, 4 * (k % 2) : 4 * (k % 2) + 4, :] = total
 
     spread_ref[...] = jnp.where((z_out >> 1) == (z_in & (HALF - 1)), 1.0, 0.0)
 
-    pl.semaphore_wait(barrier, jnp.where(owns, 2 * n_sub - 1 + n_z - 1 + 3, n_sub + 5))
-
-    for step in away:
+    pl.semaphore_wait(barrier, 8 + jnp.where(owns, 2 * n_sub - 1 + n_z - 1, n_own))
+
+    def share(number, place):
         pltpu.make_async_remote_copy(
-            src_ref=msg1.at[step[0] * inner + step[1]],
-            dst_ref=recv1.at[side * n_sub + slot(step)], send_sem=send1, recv_sem=got1,
-            device_id=(owner_g, moved(step)), device_id_type=MESH,
+            src_ref=msg1.at[number], dst_ref=recv1.at[side * n_sub + me_s],
+            send_sem=send1, recv_sem=got1,
+            device_id=(owner_g, place), device_id_type=MESH,
         ).start()
 
-    @pl.when(jnp.logical_not(owns))
-    def _():
-        pltpu.make_async_remote_copy(
-            src_ref=msg1.at[0], dst_ref=recv1.at[0], send_sem=send1, recv_sem=got1,
-            device_id=(owner_g, me_s), device_id_type=MESH,
-        ).start()
+    for number, place in enumerate(places):
+        pl.when(jnp.logical_not(owns) | (me_s != place))(functools.partial(share, number, place))
 
     for place, (a, b) in enumerate(ring):
         pltpu.make_async_remote_copy(
@@ -291,17 +295,22 @@
 
     @pl.when(owns)
     def _():
-        recv1[n_sub] = msg1[0]
-        solve_modes(
-            n_grp, n_sub, me_s, height5, weights_z, forward_ref, backward_ref, still_ref
-        )
+        recv1[n_sub + me_s] = msg1[own_index]
+        transforms(n_grp, forward_ref, backward_ref)
+        for pair in range(2):
+            wave_f = (2 * own_index + pair).astype(jnp.float32)
+            solve_modes(
+                n_grp, n_sub, wave_f, height5, weights_z.at[pair], still_ref.at[pair]
+            )
         arrived(recv1.at[pl.ds(0, 2 * n_sub - 1)], got1)
         other = jnp.sum(recv1[0:n_sub], axis=0)
         own = jnp.sum(recv1[n_sub : 2 * n_sub], axis=0)
         gap = jnp.zeros((2, LANES), jnp.float32)
-        both = jnp.concatenate([other, gap, gap], 0) + jnp.concatenate([gap, own, gap], 0)
-        msg2[...] = both
-        recv2[0] = both
+        for pair in range(2):
+            left, right = other[4 * pair : 4 * pair + 4], own[4 * pair : 4 * pair + 4]
+            both = jnp.concatenate([left, gap, gap], 0) + jnp.concatenate([gap, right, gap], 0)
+            msg2[pair] = both
+            recv2[0, pair] = both
         for step in along_z:
             pltpu.make_async_remote_copy(
                 src_ref=msg2, dst_ref=recv2.at[-step % n_z], send_sem=send2, recv_sem=got2,
@@ -309,39 +318,58 @@
             ).start()
         arrived(recv2.at[pl.ds(1, n_z - 1)], got2)
 
-        rows_in = recv2[...].reshape(8 * n_z, LANES)
-        field = matmul(forward_ref[...], rows_in)
-        column = jnp.sum(rows_in, axis=0, keepdims=True)
+        fields, means = [], []
         low_half = lax.broadcasted_iota(jnp.int32, (1, LANES), 1) < HALF
-        mean = jnp.sum(jnp.where(low_half, column, 0.0), axis=1, keepdims=True) * (1.0 / HALF)
-        field = field - still_ref[...] * mean
-        for group in range(2):
-            total = weights_z[group, REACH] * field
-            for offset in range(1, REACH + 1):
-                step = offset << (3 * group)
-                total = total + (
-                    weights_z[group, REACH - offset] * pltpu.roll(field, step, axis=1)
-                    + weights_z[group, REACH + offset] * pltpu.roll(field, LANES - step, axis=1)
-                )
-            field = total
-        lines = []
-        for r in range(6):
-            line = backward_ref[r, 0:8] * field[0:8]
-            for k in range(8, ny5, 8):
-                line = line + backward_ref[r, k : k + 8] * field[k : k + 8]
-            lines.append(jnp.sum(line, axis=0, keepdims=True))
-        msg3[0] = jnp.concatenate(lines[0:4], 0)
-        msg3[1] = jnp.concatenate(lines[2:6], 0)
-        recv3[0] = msg3[1]
-        for step in here:
-            for core in (0, 1):
-                if core == 0 or step != (0, 0):
-                    pltpu.make_async_remote_copy(
-                        src_ref=msg3.at[core], dst_ref=recv3.at[slot(step)],
-                        send_sem=send3, recv_sem=got3,
-                        device_id=(owner_g if core else other_g, moved(step)),
-                        device_id_type=MESH,
-                    ).start()
+        for pair in range(2):
+            rows_in = jnp.concatenate([recv2[k, pair] for k in range(n_z)], 0)
+            fields.append(matmul(forward_ref[...], rows_in))
+            column = jnp.where(low_half, jnp.sum(rows_in, axis=0, keepdims=True), 0.0)
+            means.append(jnp.sum(column, axis=1, keepdims=True) * (1.0 / HALF))
+        lines = [[], []]
+        for pair in range(2):
+            field = fields[pair] - still_ref[pair] * means[pair]
+            for group in range(2):
+                total = weights_z[pair, group, REACH] * field
+                for offset in range(1, REACH + 1):
+                    step = offset << (3 * group)
+                    total = total + (
+                        weights_z[pair, group, REACH - offset] * pltpu.roll(field, step, axis=1)
+                        + weights_z[pair, group, REACH + offset]
+                        * pltpu.roll(field, LANES - step, axis=1)
+                    )
+                field = total
+            for r in range(6):
+                line = backward_ref[r, 0:8] * field[0:8]
+                for k in range(8, ny5, 8):
+                    line = line + backward_ref[r, k : k + 8] * field[k : k + 8]
+                lines[pair].append(jnp.sum(line, axis=0, keepdims=True))
+        for core, first in ((0, 0), (1, 2)):
+            msg3[core] = jnp.concatenate(
+                lines[0][first : first + 4] + lines[1][first : first + 4], 0
+            )
+        recv3[own_index] = msg3[1]
+
+        def give(core, place):
+            pltpu.make_async_remote_copy(
+                src_ref=msg3.at[core], dst_ref=recv3.at[own_index],
+                send_sem=send3, recv_sem=got3,
+                device_id=(owner_g if core else other_g, place), device_id_type=MESH,
+            ).start()
+
+        in_order = sorted(range(n_sub), key=lambda p: hops((p // inner, p % inner), sizes))
+        for place in in_order:
+            pl.when(me_s != place)(functools.partial(give, 1, place))
+            give(0, place)
+
+    for j in range(4):
+        for number in range(n_own):
+            table8[j, number] = jnp.concatenate(
+                [
+                    jnp.broadcast_to(table[j, k : k + 1, :], (4, LANES))
+                    for k in (2 * number, 2 * number + 1)
+                ],
+                0,
+            )
 
     arrived(halo, halo_recv)
     big[:, 12:16, :] = jnp.zeros((12, 4, LANES), jnp.float32)
@@ -363,16 +391,17 @@
 
     @pl.when(owns)
     def _():
-        arrived(recv3.at[pl.ds(1, n_sub - 1)], got3)
+        arrived(recv3.at[pl.ds(0, n_own - 1)], got3)
 
     @pl.when(jnp.logical_not(owns))
     def _():
         arrived(recv3, got3)
 
     for j in range(4):
-        total = table[j, 0:1, :] * recv3[0]
-        for k in range(1, n_sub):
-            total = total + table[j, k : k + 1, :] * recv3[k]
+        total = table8[j, 0] * recv3[0]
+        for k in range(1, n_own):
+            total = total + table8[j, k] * recv3[k]
+        total = total[0:4] + total[4:8]
         pairs[pl.ds(2 * j, 4, stride=8), :] = total
         pairs[pl.ds(2 * j + 1, 4, stride=8), :] = total
     for j in (1, 2):
@@ -394,13 +423,13 @@
 
     @pl.when(owns)
     def _():
-        arrived(recv1.at[pl.ds(0, n_sub - 1)], send1)
+        arrived(recv1.at[pl.ds(0, n_own - 1)], send1)
         arrived(recv2.at[pl.ds(1, n_z - 1)], send2)
         arrived(recv1.at[pl.ds(0, 2 * n_sub - 1)], send3)
 
     @pl.when(jnp.logical_not(owns))
     def _():
-        arrived(recv1.at[pl.ds(0, n_sub)], send1)
+        arrived(recv1.at[pl.ds(0, n_own)], send1)
 
 
 def hand_over(cor_in, coarse_in, cor_out, coarse_out, sem1, sem2):
@@ -431,20 +460,21 @@
             pltpu.VMEM((1, LANES), f32),
             pltpu.VMEM((8, 8, LANES), f32),
             pltpu.VMEM((4, n_sub, LANES), f32),
-            pltpu.VMEM((n_sub, 4, LANES), f32),
-            pltpu.VMEM((2 * n_sub, 4, LANES), f32),
-            pltpu.VMEM((8, LANES), f32),
-            pltpu.VMEM((n_grp // 2, 8, LANES), f32),
-            pltpu.VMEM((2, 4, LANES), f32),
-            pltpu.VMEM((n_sub, 4, LANES), f32),
+            pltpu.VMEM((4, n_sub // 2, 8, LANES), f32),
+            pltpu.VMEM((n_sub // 2, 8, LANES), f32),
+            pltpu.VMEM((2 * n_sub, 8, LANES), f32),
+            pltpu.VMEM((2, 8, LANES), f32),
+            pltpu.VMEM((n_grp // 2, 2, 8, LANES), f32),
+            pltpu.VMEM((2, 8, LANES), f32),
+            pltpu.VMEM((n_sub // 2, 8, LANES), f32),
             pltpu.VMEM((8, 4, 4, LANES), f32),
             pltpu.VMEM((12, 16, LANES), f32),
             pltpu.VMEM((8, 16, LANES), f32),
             pltpu.VMEM((32, LANES), f32),
-            pltpu.VMEM((2, 2 * REACH + 1, ny5, LANES), f32),
+            pltpu.VMEM((2, 2, 2 * REACH + 1, ny5, LANES), f32),
             pltpu.VMEM((ny5, 4 * n_grp), f32),
             pltpu.VMEM((6, ny5, LANES), f32),
-            pltpu.VMEM((ny5, LANES), f32),
+            pltpu.VMEM((2, ny5, LANES), f32),
             pltpu.VMEM((LANES, LANES), f32),
         ]
         + [dma] * 10,

time: 37.5 us -> 36.9 us (0.984)
  Pallas kernels: 36.7 us -> 36.1 us
    pallas_call x1, Pallas kernels: 36 us -> 35.4 us  [on_device(): pl.pallas_call(functools.partial(kernel, n_grp, n_sub), out_shape=(pltpu....]
where the time goes in v5:
time: 36.9 us; the launch traced here: 36.7 us
  Pallas kernels  36.1 us (98%)
  between operations  0.64 us (2%)
    pallas_call x1, Pallas kernels, on_device(): pl.pallas_call(functools.partial(kernel, n_grp, n_sub), out_shape=(pltpu....  35.4 us

profile of v5, /device:TPU:1, one launch (start us, length us, event | category | flops | bytes accessed | tf_op | source)
XLA Modules:
  0.0 36.7 jit_solution(10529261453855146910)
XLA Ops:
  0.6 35.4 %shard_map.41 = (f32[4,4,128]{2,1,0:T(4,128)S(1)}, f32[2,2,64]{2,1,0:T(2,128)S(1)}) custom-call(f32[4,4,128]{2,1,0:T(4,128)} %bitcast.4, f32[1,128]{1,0:T(1,128)} %bitcast.5), custom_call_target="tpu_custom_call" | custom-call | tf_op jit(solution)/shard_map/pallas_call | solution.py:450
  36.1 0.6 %shard_map.42 = (f32[4,4,128]{2,1,0:T(4,128)}, f32[2,2,64]{2,1,0:T(2,128)}) custom-call(f32[4,4,128]{2,1,0:T(4,128)S(1)} %get-tuple-element.6.cor_in, f32[2,2,64]{2,1,0:T(2,128)S(1)} %get-tuple-element.7.coarse_in), custom_call_target="tpu_custom_call" | custom-call | tf_op jit(solution)/shard_map/pallas_call | solution.py:483

commit v6 on v5

--- a/solution.py
+++ b/solution.py
@@ -282,7 +282,7 @@
             device_id=(owner_g, place), device_id_type=MESH,
         ).start()
 
-    for number, place in enumerate(places):
+    for number, place in reversed(list(enumerate(places))):
         pl.when(jnp.logical_not(owns) | (me_s != place))(functools.partial(share, number, place))
 
     for place, (a, b) in enumerate(ring):

time: 36.9 us -> 36.2 us (0.981)
  Pallas kernels: 36.1 us -> 35.4 us
    pallas_call x1, Pallas kernels: 35.4 us -> 34.8 us  [on_device(): pl.pallas_call(functools.partial(kernel, n_grp, n_sub), out_shape=(pltpu....]
where the time goes in v6:
time: 36.2 us; the launch traced here: 36 us
  Pallas kernels  35.4 us (98%)
  between operations  0.64 us (2%)
    pallas_call x1, Pallas kernels, on_device(): pl.pallas_call(functools.partial(kernel, n_grp, n_sub), out_shape=(pltpu....  34.8 us

profile of v6, /device:TPU:1, one launch (start us, length us, event | category | flops | bytes accessed | tf_op | source)
XLA Modules:
  0.0 36.0 jit_solution(16771113821758176651)
XLA Ops:
  0.6 34.8 %shard_map.41 = (f32[4,4,128]{2,1,0:T(4,128)S(1)}, f32[2,2,64]{2,1,0:T(2,128)S(1)}) custom-call(f32[4,4,128]{2,1,0:T(4,128)} %bitcast.4, f32[1,128]{1,0:T(1,128)} %bitcast.5), custom_call_target="tpu_custom_call" | custom-call | tf_op jit(solution)/shard_map/pallas_call | solution.py:450
  35.4 0.6 %shard_map.42 = (f32[4,4,128]{2,1,0:T(4,128)}, f32[2,2,64]{2,1,0:T(2,128)}) custom-call(f32[4,4,128]{2,1,0:T(4,128)S(1)} %get-tuple-element.6.cor_in, f32[2,2,64]{2,1,0:T(2,128)S(1)} %get-tuple-element.7.coarse_in), custom_call_target="tpu_custom_call" | custom-call | tf_op jit(solution)/shard_map/pallas_call | solution.py:483

commit v7 on v6

--- a/solution.py
+++ b/solution.py
@@ -282,7 +282,12 @@
             device_id=(owner_g, place), device_id_type=MESH,
         ).start()
 
-    for number, place in reversed(list(enumerate(places))):
+    behind = (0.0, 0.4, 0.8, 1.2, 1.8, 1.7, 1.3, 1.1)
+
+    def start_of(item):
+        return 0.6 * ring_hops(item[1] // inner, outer) + behind[item[1] % 8]
+
+    for number, place in sorted(enumerate(places), key=start_of, reverse=True):
         pl.when(jnp.logical_not(owns) | (me_s != place))(functools.partial(share, number, place))
 
     for place, (a, b) in enumerate(ring):
@@ -320,10 +325,18 @@
 
         fields, means = [], []
         low_half = lax.broadcasted_iota(jnp.int32, (1, LANES), 1) < HALF
+        rows_in = jnp.concatenate(
+            [
+                jnp.concatenate([recv2[k, pair] for k in range(n_z)], 0)
+                for pair in range(2)
+            ],
+            1,
+        )
+        spectrum = matmul(forward_ref[...], rows_in)
         for pair in range(2):
-            rows_in = jnp.concatenate([recv2[k, pair] for k in range(n_z)], 0)
-            fields.append(matmul(forward_ref[...], rows_in))
-            column = jnp.where(low_half, jnp.sum(rows_in, axis=0, keepdims=True), 0.0)
+            half = slice(LANES * pair, LANES * (pair + 1))
+            fields.append(spectrum[:, half])
+            column = jnp.where(low_half, jnp.sum(rows_in[:, half], axis=0, keepdims=True), 0.0)
             means.append(jnp.sum(column, axis=1, keepdims=True) * (1.0 / HALF))
         lines = [[], []]
         for pair in range(2):

time: 36.2 us -> 35.7 us (0.986)
  Pallas kernels: 35.4 us -> 34.9 us
    pallas_call x1, Pallas kernels: 34.8 us -> 34.3 us  [on_device(): pl.pallas_call(functools.partial(kernel, n_grp, n_sub), out_shape=(pltpu....]
where the time goes in v7:
time: 35.7 us; the launch traced here: 35.5 us
  Pallas kernels  34.9 us (98%)
  between operations  0.64 us (2%)
    pallas_call x1, Pallas kernels, on_device(): pl.pallas_call(functools.partial(kernel, n_grp, n_sub), out_shape=(pltpu....  34.3 us

profile of v7, /device:TPU:1, one launch (start us, length us, event | category | flops | bytes accessed | tf_op | source)
XLA Modules:
  0.0 35.5 jit_solution(6862102428057960434)
XLA Ops:
  0.6 34.3 %shard_map.41 = (f32[4,4,128]{2,1,0:T(4,128)S(1)}, f32[2,2,64]{2,1,0:T(2,128)S(1)}) custom-call(f32[4,4,128]{2,1,0:T(4,128)} %bitcast.4, f32[1,128]{1,0:T(1,128)} %bitcast.5), custom_call_target="tpu_custom_call" | custom-call | tf_op jit(solution)/shard_map/pallas_call | solution.py:463
  34.9 0.6 %shard_map.42 = (f32[4,4,128]{2,1,0:T(4,128)}, f32[2,2,64]{2,1,0:T(2,128)}) custom-call(f32[4,4,128]{2,1,0:T(4,128)S(1)} %get-tuple-element.6.cor_in, f32[2,2,64]{2,1,0:T(2,128)S(1)} %get-tuple-element.7.coarse_in), custom_call_target="tpu_custom_call" | custom-call | tf_op jit(solution)/shard_map/pallas_call | solution.py:496

commit v8 on v7

--- a/solution.py
+++ b/solution.py
@@ -260,7 +260,7 @@
     z_in = lax.broadcasted_iota(jnp.int32, (LANES, LANES), 0)
     z_out = lax.broadcasted_iota(jnp.int32, (LANES, LANES), 1)
     gather_z = jnp.where((z_in >> 1) == (z_out & (HALF - 1)), 1.0, 0.0)
-    pairs[...] = matmul(row_pairs, 0.25 * gather_z)
+    pairs[0:32, :] = matmul(row_pairs, 0.25 * gather_z)
     parts = [
         pairs[pl.ds(2 * j, 4, stride=8), :] + pairs[pl.ds(2 * j + 1, 4, stride=8), :]
         for j in range(4)
@@ -420,7 +420,7 @@
     for j in (1, 2):
         both = pairs[pl.ds(8 * j + 2, 2, stride=2), :]
         coarse_ref[j - 1] = (both + pltpu.roll(both, HALF, axis=1))[:, 0:HALF]
-    coarse = matmul(pairs[...], spread_ref[...])
+    coarse = matmul(pairs[0:32, :], spread_ref[...])
     lifted = smooth + jnp.concatenate(
         [coarse[8 * (j // 2) : 8 * (j // 2) + 8][None] for j in range(8)], 0
     )
@@ -483,7 +483,7 @@
             pltpu.VMEM((8, 4, 4, LANES), f32),
             pltpu.VMEM((12, 16, LANES), f32),
             pltpu.VMEM((8, 16, LANES), f32),
-            pltpu.VMEM((32, LANES), f32),
+            pltpu.VMEM((80, LANES), f32),
             pltpu.VMEM((2, 2, 2 * REACH + 1, ny5, LANES), f32),
             pltpu.VMEM((ny5, 4 * n_grp), f32),
             pltpu.VMEM((6, ny5, LANES), f32),

time: 35.7 us -> 35.7 us (level)
  no operation moved by 1% of the time
where the time goes in v8:
time: 35.7 us; the launch traced here: 35.5 us
  Pallas kernels  34.9 us (98%)
  between operations  0.64 us (2%)
    pallas_call x1, Pallas kernels, on_device(): pl.pallas_call(functools.partial(kernel, n_grp, n_sub), out_shape=(pltpu....  34.3 us

profile of v8, /device:TPU:1, one launch (start us, length us, event | category | flops | bytes accessed | tf_op | source)
XLA Modules:
  0.0 35.5 jit_solution(9347256352173537605)
XLA Ops:
  0.6 34.3 %shard_map.41 = (f32[4,4,128]{2,1,0:T(4,128)S(1)}, f32[2,2,64]{2,1,0:T(2,128)S(1)}) custom-call(f32[4,4,128]{2,1,0:T(4,128)} %bitcast.4, f32[1,128]{1,0:T(1,128)} %bitcast.5), custom_call_target="tpu_custom_call" | custom-call | tf_op jit(solution)/shard_map/pallas_call | solution.py:463
  34.9 0.6 %shard_map.42 = (f32[4,4,128]{2,1,0:T(4,128)}, f32[2,2,64]{2,1,0:T(2,128)}) custom-call(f32[4,4,128]{2,1,0:T(4,128)S(1)} %get-tuple-element.6.cor_in, f32[2,2,64]{2,1,0:T(2,128)S(1)} %get-tuple-element.7.coarse_in), custom_call_target="tpu_custom_call" | custom-call | tf_op jit(solution)/shard_map/pallas_call | solution.py:496

commit v9 on v8

--- a/solution.py
+++ b/solution.py
@@ -316,11 +316,15 @@
             both = jnp.concatenate([left, gap, gap], 0) + jnp.concatenate([gap, right, gap], 0)
             msg2[pair] = both
             recv2[0, pair] = both
-        for step in along_z:
+        def pass_on(plane):
             pltpu.make_async_remote_copy(
-                src_ref=msg2, dst_ref=recv2.at[-step % n_z], send_sem=send2, recv_sem=got2,
-                device_id=(2 * ((me_z + step) % n_z) + 1, me_s), device_id_type=MESH,
+                src_ref=msg2, dst_ref=recv2.at[(me_z - plane + n_z) % n_z],
+                send_sem=send2, recv_sem=got2,
+                device_id=(2 * plane + 1, me_s), device_id_type=MESH,
             ).start()
+
+        for plane in range(n_z):
+            pl.when(me_z != plane)(functools.partial(pass_on, plane))
         arrived(recv2.at[pl.ds(1, n_z - 1)], got2)
 
         fields, means = [], []

time: 35.7 us -> 36.2 us (1.014)
  the two profiles are of different devices: /device:TPU:1 before, /device:TPU:28 now
where the time goes in v9:
time: 36.2 us; the launch traced here: 36 us
  Pallas kernels  35.4 us (98%)
  between operations  0.64 us (2%)
    pallas_call x1, Pallas kernels, on_device(): pl.pallas_call(functools.partial(kernel, n_grp, n_sub), out_shape=(pltpu....  34.7 us

profile of v9, /device:TPU:28, one launch (start us, length us, event | category | flops | bytes accessed | tf_op | source)
XLA Modules:
  0.0 36.0 jit_solution(3203152530607827319)
XLA Ops:
  0.6 34.7 %shard_map.41 = (f32[4,4,128]{2,1,0:T(4,128)S(1)}, f32[2,2,64]{2,1,0:T(2,128)S(1)}) custom-call(f32[4,4,128]{2,1,0:T(4,128)} %bitcast.4, f32[1,128]{1,0:T(1,128)} %bitcast.5), custom_call_target="tpu_custom_call" | custom-call | tf_op jit(solution)/shard_map/pallas_call | solution.py:467
  35.4 0.6 %shard_map.42 = (f32[4,4,128]{2,1,0:T(4,128)}, f32[2,2,64]{2,1,0:T(2,128)}) custom-call(f32[4,4,128]{2,1,0:T(4,128)S(1)} %get-tuple-element.6.cor_in, f32[2,2,64]{2,1,0:T(2,128)S(1)} %get-tuple-element.7.coarse_in), custom_call_target="tpu_custom_call" | custom-call | tf_op jit(solution)/shard_map/pallas_call | solution.py:500
